TPU v7x, 32 devices: a whole 2x2x4 slice. The times are simulated.
32 devices in a mesh: tile: 8 (over z, y), slab: 4 (over x, core).
Axes of the slice: x: 2, y: 2, z: 4, core: 2. Of those that a mesh axis runs over, the one named last changes fastest.
Arguments:
- voxel_cell: int32 [12288, 128], P(('tile', 'slab')), may hold values from 0 to 255
- offsets: float32 [12288, 2, 128], P(('tile', 'slab')), may hold values from 0 to 1
- line_center: float32 [12288, 128], P(('tile', 'slab')), may hold values from 0 to 128
- line_width: float32 [12288, 128], P(('tile', 'slab')), may hold values from 1 to 12
- luminosity: float32 [12288, 128], P(('tile', 'slab')), may hold values from 0.3 to 8
- block_rows: int32 [12288], P(('tile', 'slab')), may hold values from 1 to 128, as said below
- block_chan: int32 [12288], P(('tile', 'slab')), may hold values from 0 to 31, as said below
- slot_table: int32 [32, 768], P(('tile', 'slab')), may hold values from -1 to 383, as said below
- beam_width: float32 [4096], P('slab'), may hold values from 0.6 to 3
- spectral_taps: float32 [31], replicated, may hold values from -3 to 3
Outputs:
- sky_cube: float32 [8, 256, 4096], P('tile', None, 'slab')
Inputs may be any that keep to these rules, and one draw needn't show every extreme that they name: `slot_table`: row i lists the blocks of device i: entry j belongs to destination device j // 24, that is field j // 24 // 4 and slab j // 24 % 4, and holds a local block index or -1 for an empty slot. Every local block stands in exactly one entry of its row. In every draw some destination receives 24 blocks from every device. `block_chan`: A block listed for a destination of slab s has its channel block in s * 8 .. (s + 1) * 8 - 1. Rows 0 .. block_rows - 1 of a block are emitters, the others padding.
All inputs are finite; a program needn't handle non-finite values.
Results may differ from a plain program's by a relative error of at most 0.0045.
Values sent between devices are 32-bit elements; how exact they have to be, the bound alone decides.
No kernel may reach another device: no remote copies, remote signals or barrier semaphores. Data moves between devices by JAX's collectives and lax.ppermute only.
A program may use at most 64 MiB of HBM per device.

v0:
```python
import functools
import math

import jax
import jax.numpy as jnp
from jax import lax
from jax.experimental import pallas as pl
from jax.experimental.pallas import tpu as pltpu
from jax.sharding import PartitionSpec as P

SIDE = 16
PIX = SIDE * SIDE
CB = 128
ROWS = 128
TAPS = 31
HALF = 15
EDGE = 16
NCB = 32
FIELDS = 6
UNROLL = 6
LOG2E = math.log2(math.e)
SMEM = pl.BlockSpec(memory_space=pltpu.SMEM)
VMEM = pl.BlockSpec(memory_space=pltpu.VMEM)
ANY = pl.BlockSpec(memory_space=pl.ANY)


def chunk_sizes(per_dest):
    part = max(per_dest * 3 // 8, 1)
    sizes = [part, part, per_dest - 2 * part]
    return [size for size in sizes if size > 0]


def padded_rows(rows):
    return -(-rows // 8) * 8


def pack_kernel(sizes, slab_count, share, slot_ref, count_ref, chan_ref, cell_ref, offset_ref, center_ref,
                width_ref, lum_ref, *refs):
    outs, (props, stream) = refs[: len(sizes)], refs[len(sizes) :]
    dest_count = outs[0].shape[0]
    per_dest = sum(sizes)
    lane = lax.broadcasted_iota(jnp.int32, (8, ROWS), 1)
    row_lane = lax.broadcasted_iota(jnp.int32, (1, ROWS), 1)

    def gather_fields(tile, carry):
        first = pl.multiple_of(tile * 8, 8)
        here = pl.ds(first, 8)
        fields = (
            cell_ref[here, :].astype(jnp.float32),
            offset_ref[pl.ds(2 * first, 8, stride=2), :],
            offset_ref[pl.ds(2 * first + 1, 8, stride=2), :],
            center_ref[here, :],
            (-0.5 * LOG2E) / jnp.square(width_ref[here, :]),
            lum_ref[here, :].astype(jnp.bfloat16).astype(jnp.float32),
        )
        for field, values in enumerate(fields):
            props[pl.ds(8 * first + field, 8, stride=8), :] = values
        return carry

    lax.fori_loop(0, cell_ref.shape[0] // 8, gather_fields, 0, unroll=2)

    def one_dest(dest, longest):
        first_chan = lax.rem(dest, slab_count) * share
        chan_row = jnp.zeros((1, ROWS), jnp.int32)
        end_row = jnp.zeros((1, ROWS), jnp.int32)
        start = jnp.int32(0)
        for slot in range(per_dest):
            block = slot_ref[0, dest * per_dest + slot]
            filled = block >= 0
            block = jnp.maximum(block, 0)
            live = jnp.where(filled, count_ref[block], 0)
            chan_row = jnp.where(row_lane == slot, chan_ref[block], chan_row)
            shift = start & (ROWS - 1)
            group = start >> 7
            turned = pltpu.roll(props[pl.ds(pl.multiple_of(block * 8, 8), 8), :], shift, 1)
            pltpu.store(stream.at[group], turned, mask=lane >= shift)
            stream[group + 1] = turned
            start = start + live
            end_row = jnp.where(row_lane == slot, start, end_row)
        group = 0
        for out, size in zip(outs, sizes):
            for place in range(size):
                out[dest, place * FIELDS : (place + 1) * FIELDS, :] = stream[group, 0:FIELDS, :]
                group += 1
        meta = sizes[0] * FIELDS
        outs[0][dest, meta : meta + 1, :] = (chan_row - first_chan).astype(jnp.float32)
        outs[0][dest, meta + 1 : meta + 2, :] = end_row.astype(jnp.float32)
        return jnp.maximum(longest, start)

    longest = lax.fori_loop(0, dest_count, one_dest, jnp.int32(0))
    meta = sizes[0] * FIELDS

    def tell(dest, carry):
        row = outs[0][dest, meta : meta + 1, :]
        outs[0][dest, meta : meta + 1, :] = jnp.where(row_lane == ROWS - 1, longest.astype(jnp.float32), row)
        return carry

    lax.fori_loop(0, dest_count, tell, 0)


def pack(sizes, dest_count, slab_count, share, slot_list, counts, chans, cells, offsets, centers, widths, lums):
    rows = [size * FIELDS for size in sizes]
    rows[0] += 2
    block_total = cells.shape[0]
    return pl.pallas_call(
        functools.partial(pack_kernel, sizes, slab_count, share),
        out_shape=[jax.ShapeDtypeStruct((dest_count, padded_rows(r), ROWS), jnp.float32) for r in rows],
        in_specs=[SMEM] * 3 + [VMEM] * 5,
        out_specs=[VMEM] * len(sizes),
        scratch_shapes=[
            pltpu.VMEM((block_total * 8, ROWS), jnp.float32),
            pltpu.VMEM((sum(sizes) + 2, 8, ROWS), jnp.float32),
        ],
        name="pack",
    )(slot_list, counts, chans, cells, offsets.reshape(block_total * 2, ROWS), centers, widths, lums)


def exclusive(size):
    before = lax.broadcasted_iota(jnp.int32, (size, size), 0)
    return (before < lax.broadcasted_iota(jnp.int32, (size, size), 1)).astype(jnp.bfloat16)


def plan_moves(size, first, per_dest, share, stride, rows, chan, end, plan):
    sources = chan.shape[0]
    lane = lax.broadcasted_iota(jnp.int32, chan.shape, 1)
    low, high = float(first * ROWS), float((first + size) * ROWS)
    start = jnp.where(lane == 0, 0.0, pltpu.roll(end, 1, 1))
    begin = jnp.clip(start, low, high) - low
    count = jnp.where(lane < per_dest, jnp.clip(end, low, high) - low - begin, 0.0)
    chan = jnp.where(count > 0.0, chan, 0.0)
    across = exclusive(ROWS)
    down = exclusive(sources)
    filled = jnp.zeros(chan.shape, jnp.float32)
    totals = jnp.zeros(chan.shape, jnp.float32)
    for c in range(share):
        own = jnp.where(chan == float(c), count, 0.0)
        moved = own.astype(jnp.bfloat16)
        here = jnp.dot(moved, across, preferred_element_type=jnp.float32)
        above = lax.dot_general(down, moved, (((0,), (0,)), ((), ())), preferred_element_type=jnp.float32)
        above = jnp.sum(above, axis=1, keepdims=True) + float(c * stride * ROWS)
        filled = filled + jnp.where(chan == float(c), here + above, 0.0)
        total = jnp.sum(jnp.sum(own, axis=0, keepdims=True), axis=1, keepdims=True)
        totals = totals + jnp.where(lane == c, total, 0.0)
    filled = filled.astype(jnp.int32)
    begin = begin.astype(jnp.int32)
    base = lax.broadcasted_iota(jnp.int32, chan.shape, 0) * rows
    group = jnp.minimum(begin >> 7, size - 1)
    table = totals.astype(jnp.int32)
    for values in ((filled >> 7) * 8, (filled - begin) & (ROWS - 1), begin & (ROWS - 1), base + group * FIELDS):
        table = jnp.where(lane < per_dest, values, pltpu.roll(table, per_dest, 1))
    plan[...] = table


def add_emitters(size, first, per_dest, chan, end, got, acc, streams, todo, plan, moves, sem):
    source_count = chan.shape[0]
    share = acc.shape[0]
    stride = streams.shape[0] // (8 * share)
    lane = lax.broadcasted_iota(jnp.int32, (FIELDS, ROWS), 1)
    plan_moves(size, first, per_dest, share, stride, (got.shape[0] - 8) // source_count, chan, end, plan)
    copy = pltpu.make_async_copy(plan, moves, sem)
    copy.start()
    copy.wait()

    def append(source, carry):
        for place in range(per_dest):
            row, begin, turn, target = (moves[source, k * per_dest + place] for k in range(4))
            target = pl.multiple_of(target, 8)
            here = got[pl.ds(row, FIELDS), :]
            there = got[pl.ds(row + FIELDS, FIELDS), :]
            filled = (jnp.full(lane.shape, begin, jnp.int32) + turn) & (ROWS - 1)
            whole = pltpu.roll(jnp.where(lane >= begin, here, there), turn, 1)
            pltpu.store(streams.at[pl.ds(target, FIELDS), :], whole, mask=lane >= filled)
            streams[pl.ds(target + 8, FIELDS), :] = whole
        return carry

    lax.fori_loop(0, source_count, append, 0)

    def list_chan(chan, count):
        total = moves[0, 4 * per_dest + chan]

        def list_pair(pair, at):
            todo[0, at] = chan
            todo[1, at] = chan * stride + 2 * pair
            todo[2, at] = total - 2 * ROWS * pair
            return at + 1

        return lax.fori_loop(0, (total + 2 * ROWS - 1) >> 8, list_pair, count)

    pair_count = lax.fori_loop(0, share, list_chan, 0)
    for extra in range(UNROLL - 1):
        todo[0, pair_count + extra] = 0
        todo[1, pair_count + extra] = 0
        todo[2, pair_count + extra] = 0

    place16 = lax.broadcasted_iota(jnp.int32, (SIDE, ROWS), 0).astype(jnp.float32)
    place8 = lax.broadcasted_iota(jnp.int32, (8, ROWS), 0).astype(jnp.float32) + 0.5

    def hat(cell, frac):
        apart = place16 - cell
        return jnp.where(apart == 0.0, 1.0 - frac, jnp.where(apart == 1.0, frac, 0.0))

    def factors(group, left):
        props = jnp.where(lane < left, streams[pl.ds(pl.multiple_of(group * 8, 8), FIELDS), :], 0.0)
        cell, frac_x, frac_y, center, decay, bright = (props[f : f + 1, :] for f in range(FIELDS))
        cell_x = jnp.floor(cell * (1.0 / SIDE))
        weight_x = hat(cell_x, frac_x)
        weight_y = hat(cell - SIDE * cell_x, frac_y)
        spread = jnp.concatenate(
            [(weight_x[x : x + 1, :] * weight_y).astype(jnp.bfloat16) for x in range(SIDE)], axis=0
        )
        apart = place8 - center
        profile = [jnp.exp2(jnp.square(apart + 8.0 * i) * decay) for i in range(CB // 8)]
        total = profile[0]
        for part in profile[1:]:
            total = total + part
        scale = bright / jnp.sum(total, axis=0, keepdims=True)
        line = jnp.concatenate(profile, axis=0) * scale
        return spread, line.astype(jnp.bfloat16)

    def some_pairs(turn, carry):
        for step in range(UNROLL):
            at = turn * UNROLL + step
            chan, group, left = todo[0, at], todo[1, at], todo[2, at]
            spread_0, line_0 = factors(group, left)
            spread_1, line_1 = factors(group + 1, left - ROWS)
            acc[chan] += lax.dot_general(
                jnp.concatenate([spread_0, spread_1], axis=1),
                jnp.concatenate([line_0, line_1], axis=1),
                (((1,), (1,)), ((), ())),
                preferred_element_type=jnp.float32,
            )
        return carry

    lax.fori_loop(0, (pair_count + UNROLL - 1) // UNROLL, some_pairs, 0)


def fetch(got_ref, got, sem):
    copy = pltpu.make_async_copy(got_ref, got.at[pl.ds(0, got_ref.shape[0])], sem)
    copy.start()
    return copy


def first_kernel(size, per_dest, share, got_ref, acc, got, got_sem, *scratch):
    copy = fetch(got_ref, got, got_sem)
    acc[...] = jnp.zeros_like(acc)
    sources = scratch[-2].shape[0]
    rows = got_ref.shape[0] // sources
    copy.wait()
    chan = got[pl.ds(size * FIELDS, sources, stride=rows), :]
    end = got[pl.ds(size * FIELDS + 1, sources, stride=rows), :]
    add_emitters(size, 0, per_dest, chan, end, got, acc, *scratch)


def more_kernel(size, first, per_dest, chan_ref, end_ref, got_ref, held_ref, acc, got, got_sem, *scratch):
    copy = fetch(got_ref, got, got_sem)
    acc[...] = held_ref[...]
    copy.wait()
    add_emitters(size, first, per_dest, chan_ref[...], end_ref[...], got, acc, *scratch)


def last_kernel(size, first, per_dest, chan_ref, end_ref, got_ref, held_ref, width_ref, cube_ref, head_ref, tail_ref,
                acc, got, got_sem, *scratch):
    copy = fetch(got_ref, got, got_sem)
    acc[...] = held_ref[...]
    copy.wait()
    add_emitters(size, first, per_dest, chan_ref[...], end_ref[...], got, acc, *scratch)
    share = acc.shape[0]

    def one_chan(chan, carry):
        columns = pl.ds(pl.multiple_of(chan * CB, CB), CB)
        smooth(acc.at[chan], width_ref[:, columns], cube_ref, columns)
        return carry

    lax.fori_loop(0, share, one_chan, 0)
    head_ref[...] = cube_ref[:, :CB].T[:EDGE]
    tail_ref[...] = cube_ref[:, (share - 1) * CB :].T[CB - EDGE :]


def smooth(plane_ref, widths, cube_ref, columns):
    decay = (-0.5 * LOG2E) / jnp.square(widths)
    places = lax.broadcasted_iota(jnp.int32, (SIDE, CB), 0).astype(jnp.float32)
    beam = [jnp.exp2(jnp.square(places - float(v)) * decay) for v in range(SIDE)]
    norm = beam[0]
    for v in range(1, SIDE):
        norm = norm + beam[v]
    inverse = 1.0 / norm
    beam = [b * inverse for b in beam]
    half = SIDE // 2
    even, odd = [None] * half, [None] * half
    for v in range(half):
        low = plane_ref[v * SIDE : (v + 1) * SIDE, :]
        high = plane_ref[(SIDE - 1 - v) * SIDE : (SIDE - v) * SIDE, :]
        both, apart = low + high, low - high
        near, far = beam[v][:half], beam[SIDE - 1 - v][:half]
        mean, rest = 0.5 * (near + far), 0.5 * (near - far)
        for x in range(half):
            term_even, term_odd = mean[x : x + 1, :] * both, rest[x : x + 1, :] * apart
            even[x] = term_even if v == 0 else even[x] + term_even
            odd[x] = term_odd if v == 0 else odd[x] + term_odd
    for x in range(SIDE):
        along_x = even[x] + odd[x] if x < half else even[SIDE - 1 - x] - odd[SIDE - 1 - x]
        total = None
        for v in range(SIDE):
            term = beam[v] * along_x[v : v + 1, :]
            total = term if v == 0 else total + term
        cube_ref[x * SIDE : (x + 1) * SIDE, columns] = total


def emitter_scratch(size, got, share):
    sources, rows = got.shape[:2]
    work = size * sources
    return [
        pltpu.VMEM((sources * rows + 8, ROWS), jnp.float32),
        pltpu.SemaphoreType.DMA,
        pltpu.VMEM((share * (work + 2) * 8, ROWS), jnp.float32),
        pltpu.SMEM((3, work // 2 + share + UNROLL), jnp.int32),
        pltpu.VMEM((sources, ROWS), jnp.int32),
        pltpu.SMEM((sources, ROWS), jnp.int32),
        pltpu.SemaphoreType.DMA,
    ]


def flat(got):
    return got.reshape(-1, ROWS)


def emitter_cost(size, got):
    work = size * got.shape[0]
    return pl.CostEstimate(
        flops=work * 2 * PIX * CB * ROWS, transcendentals=work * CB * ROWS, bytes_accessed=got.size * 4
    )


def deposit_first(size, per_dest, share, got):
    return pl.pallas_call(
        functools.partial(first_kernel, size, per_dest, share),
        out_shape=jax.ShapeDtypeStruct((share, PIX, CB), jnp.float32),
        in_specs=[ANY],
        out_specs=VMEM,
        scratch_shapes=emitter_scratch(size, got, share),
        cost_estimate=emitter_cost(size, got),
        name="deposit_first",
    )(flat(got))


def deposit_more(size, first, per_dest, share, chan, end, got, held):
    return pl.pallas_call(
        functools.partial(more_kernel, size, first, per_dest),
        out_shape=jax.ShapeDtypeStruct((share, PIX, CB), jnp.float32),
        in_specs=[VMEM, VMEM, ANY, VMEM],
        out_specs=VMEM,
        scratch_shapes=emitter_scratch(size, got, share),
        input_output_aliases={3: 0},
        name="deposit_more",
    )(chan, end, flat(got), held)


def deposit_last(size, first, per_dest, share, chan, end, got, held, widths):
    edge = jax.ShapeDtypeStruct((EDGE, PIX), jnp.float32)
    return pl.pallas_call(
        functools.partial(last_kernel, size, first, per_dest),
        out_shape=[jax.ShapeDtypeStruct((PIX, share * CB), jnp.float32), edge, edge],
        in_specs=[VMEM, VMEM, ANY, VMEM, VMEM],
        out_specs=[VMEM] * 3,
        scratch_shapes=[pltpu.VMEM((share, PIX, CB), jnp.float32)] + emitter_scratch(size, got, share),
        cost_estimate=emitter_cost(size, got),
        name="deposit_last",
    )(chan, end, flat(got), held, widths.reshape(1, -1))


def split(values):
    high = values.astype(jnp.bfloat16)
    return high, (values - high.astype(jnp.float32)).astype(jnp.bfloat16)


def times(left, right, dims):
    (left_high, left_low), (right_high, right_low) = left, right

    def dot(a, b):
        return lax.dot_general(a, b, (dims, ((), ())), preferred_element_type=jnp.float32)

    return dot(left_high, right_high) + (dot(left_high, right_low) + dot(left_low, right_high))


def band_kernel(taps_ref, high_ref, low_ref):
    rows, columns = high_ref.shape
    apart = lax.broadcasted_iota(jnp.int32, (3 * CB, CB), 0) - lax.broadcasted_iota(jnp.int32, (3 * CB, CB), 1)
    band = jnp.zeros((3 * CB, CB), jnp.float32)
    for k in range(TAPS):
        band = jnp.where(apart == CB - HALF + k, taps_ref[k], band)
    high, low = split(band)
    high_ref[...] = jnp.zeros_like(high_ref)
    low_ref[...] = jnp.zeros_like(low_ref)
    for i in range(columns // CB):
        high_ref[i * CB : (i + 3) * CB, i * CB : (i + 1) * CB] = high
        low_ref[i * CB : (i + 3) * CB, i * CB : (i + 1) * CB] = low


def bands(taps, wide):
    return pl.pallas_call(
        band_kernel,
        out_shape=[jax.ShapeDtypeStruct((wide + 2 * CB, wide), jnp.bfloat16)] * 2,
        in_specs=[SMEM],
        out_specs=[VMEM] * 2,
        name="bands",
    )(taps)


def taps_kernel(high_ref, low_ref, cube_ref, out_ref):
    wide = high_ref.shape[1]
    end = cube_ref.shape[1]
    for start in range(0, end, wide):
        low, high = max(start - CB, 0), min(start + wide + CB, end)
        rows = slice(low - start + CB, high - start + CB)
        out_ref[:, start : start + wide] = times(
            split(cube_ref[:, low:high]), (high_ref[rows], low_ref[rows]), ((1,), (0,))
        )


def sum_taps(band, cube):
    return pl.pallas_call(
        taps_kernel,
        out_shape=jax.ShapeDtypeStruct(cube.shape, jnp.float32),
        in_specs=[VMEM] * 3,
        out_specs=VMEM,
        cost_estimate=pl.CostEstimate(
            flops=6 * cube.size * band[0].shape[0], transcendentals=0, bytes_accessed=cube.size * 8
        ),
        name="taps",
    )(*band, cube)


def edge_kernel(high_ref, low_ref, before_ref, after_ref, part_ref, out_ref):
    side = pl.program_id(0)
    edge = jnp.where(side == 0, before_ref[...], after_ref[...])
    out_ref[...] = part_ref[...] + times(split(edge), (high_ref[...], low_ref[...]), ((0,), (0,)))


def add_edges(band, before, after, part):
    last = part.shape[1] // CB - 1
    rows, columns = band[0].shape
    top, bottom = (CB - EDGE) // EDGE, (rows - CB) // EDGE
    corner = pl.BlockSpec((EDGE, CB), lambda i: (top + i * (bottom - top), i * (columns // CB - 1)))
    edge = pl.BlockSpec((EDGE, PIX), lambda i: (0, 0))
    block = pl.BlockSpec((PIX, CB), lambda i: (0, i * last))
    return pl.pallas_call(
        edge_kernel,
        out_shape=jax.ShapeDtypeStruct(part.shape, jnp.float32),
        grid=(2,),
        in_specs=[corner, corner, edge, edge, block],
        out_specs=block,
        input_output_aliases={4: 0},
        name="edges",
    )(*band, before, after, part)


def body(
    voxel_cell,
    offsets,
    line_center,
    line_width,
    luminosity,
    block_rows,
    block_chan,
    slot_table,
    beam_width,
    spectral_taps,
):
    slab_count = lax.axis_size("slab")
    dest_count = lax.axis_size("tile") * slab_count
    per_dest = slot_table.shape[1] // dest_count
    share = NCB // slab_count
    sizes = chunk_sizes(per_dest)
    sent = pack(
        sizes, dest_count, slab_count, share, slot_table, block_rows, block_chan,
        voxel_cell, offsets, line_center, line_width, luminosity,
    )
    def exchange(piece):
        return lax.all_to_all(piece, ("tile", "slab"), split_axis=0, concat_axis=0, tiled=True)

    got_first = exchange(sent[0])
    got_first, last_piece = lax.optimization_barrier((got_first, sent[1]))
    got_last = exchange(last_piece)
    chan = got_first[:, sizes[0] * FIELDS, :]
    end = got_first[:, sizes[0] * FIELDS + 1, :]
    band = bands(spectral_taps, 2 * CB if share % 2 == 0 else CB)
    held = deposit_first(sizes[0], per_dest, share, got_first)
    reach = sizes[0] + sizes[1]
    if len(sizes) > 2:
        longest = jnp.max(chan[:, ROWS - 1])
        held, got_last = lax.optimization_barrier((held, got_last))
        held = lax.cond(
            longest > float(reach * ROWS),
            lambda held: deposit_more(sizes[2], reach, per_dest, share, chan, end, exchange(sent[2]), held),
            lambda held: held,
            held,
        )
    cube, head, tail = deposit_last(sizes[1], sizes[0], per_dest, share, chan, end, got_last, held, beam_width)
    ends = slab_count - 1
    before = lax.ppermute(tail, "slab", [(i, i + 1) for i in range(ends)])
    after = lax.ppermute(head, "slab", [(i + 1, i) for i in range(ends)])
    return add_edges(band, before, after, sum_taps(band, cube))[None]


def solution(mesh):
    placed = (
        P(("tile", "slab"), None),
        P(("tile", "slab"), None, None),
        P(("tile", "slab"), None),
        P(("tile", "slab"), None),
        P(("tile", "slab"), None),
        P(("tile", "slab")),
        P(("tile", "slab")),
        P(("tile", "slab"), None),
        P("slab"),
        P(),
    )
    return jax.shard_map(
        body, mesh=mesh, in_specs=placed, out_specs=P("tile", None, "slab"), check_vma=False
    )
```

profile of v0, /device:TPU:13, one launch (start us, length us, event | category | flops | bytes accessed | tf_op | source)
XLA Modules:
  0.0 96.4 jit_solution(15171740103837487704)
XLA Ops:
  0.0 8.4 %pack.1 = (f32[32,56,128]{2,1,0:T(8,128)}, f32[32,56,128]{2,1,0:T(8,128)}, f32[32,40,128]{2,1,0:T(8,128)S(1)}) custom-call(s32[1,768]{1,0:T(1,128)} %slot_ref.1, s32[384]{0:T(512)} %count_ref.1, s32[384]{0:T(512)} %chan_ref.1, s32[384,128]{1,0:T(8,128)} %cell_ref.1, f32[768,128]{1,0:T(8,128)} %bitcast.13, f32[384,128]{1,0:T(8,128)} %center_ref.1, ...), custom_call_target="tpu_custom_call" | custom-call | tf_op jit(solution)/shard_map/pack/pallas_call | solution.py:105
  8.4 27.3 %all_to_all.15 = f32[32,56,128]{2,1,0:T(8,128)S(1)} all-to-all(f32[32,56,128]{2,1,0:T(8,128)} %get-tuple-element.35), channel_id=1, replica_groups=mesh['tile'=8,'slab'=4] {'tile','slab'}, dimensions={0} | all-to-all | bytes 1835008 | tf_op jit(solution)/shard_map/all_to_all | solution.py:479
  35.7 0.0 copy-start
  35.7 6.0 %all-to-all-start.2 = ((f32[32,56,128]{2,1,0:T(8,128)}), f32[32,56,128]{2,1,0:T(8,128)S(1)}, u32[]{:S(2)}, u32[]{:S(2)}) async-start(f32[32,56,128]{2,1,0:T(8,128)} %get-tuple-element.38), calls=%async_computation.2 | async-start | bytes 1835008 | tf_op jit(solution)/shard_map/all_to_all | solution.py:479
  41.7 1.7 %bands.1 = (bf16[512,256]{1,0:T(8,128)(2,1)}, bf16[512,256]{1,0:T(8,128)(2,1)}) custom-call(f32[31]{0:T(128)} %taps_ref.1), custom_call_target="tpu_custom_call" | custom-call | tf_op jit(solution)/shard_map/bands/pallas_call | solution.py:400
  43.4 0.0 copy-done
  43.4 0.2 copy.16
  43.6 0.6 slice_reduce_fusion
  44.8 21.8 %deposit_first.1 = f32[8,256,128]{2,1,0:T(8,128)S(1)} custom-call(f32[1792,128]{1,0:T(8,128)} %bitcast.10), custom_call_target="tpu_custom_call" | custom-call | flops 2415919104 | bytes 917504 | tf_op jit(solution)/shard_map/deposit_first/pallas_call | solution.py:335
  66.6 0.0 all-to-all-done.2
  66.6 0.0 copy-start.1
  66.6 0.9 copy-done.1
  67.5 16.2 %deposit_last.1 = (f32[256,1024]{1,0:T(8,128)}, f32[16,256]{1,0:T(8,128)}, f32[16,256]{1,0:T(8,128)}) custom-call(f32[32,128]{1,0:T(8,128)S(1)} %get-tuple-element.46.chan_ref, f32[32,128]{1,0:T(8,128)S(1)} %get-tuple-element.45.end_ref, f32[1792,128]{1,0:T(8,128)} %bitcast.12, f32[8,256,128]{2,1,0:T(8,128)S(1)} %get-tuple-element.47.held_ref, ...), custom_call_target="tpu_custom_call" | custom-call | flops 2415919104 | bytes 917504 | tf_op jit(solution)/shard_map/deposit_last/pallas_call | solution.py:360
  83.7 4.0 %collective-permute-start = (f32[16,256]{1,0:T(8,128)}, f32[16,256]{1,0:T(8,128)S(1)}, u32[]{:S(2)}, u32[]{:S(2)}) collective-permute-start(f32[16,256]{1,0:T(8,128)} %get-tuple-element.42), channel_id=1, source_target_pairs={{0,1},{1,2},{2,3},{4,5},{5,6},{6,7},{8,9},{9,10},{10,11},{12,13},{... | collective-permute-start | bytes 49160 | tf_op jit(solution)/shard_map/ppermute | solution.py:500
  87.7 1.9 %collective-permute-start.1 = (f32[16,256]{1,0:T(8,128)}, f32[16,256]{1,0:T(8,128)S(1)}, u32[]{:S(2)}, u32[]{:S(2)}) collective-permute-start(f32[16,256]{1,0:T(8,128)} %get-tuple-element.43), channel_id=1, source_target_pairs={{1,0},{2,1},{3,2},{5,4},{6,5},{7,6},{9,8},{10,9},{11,10},{13,12},{... | collective-permute-start | bytes 49160 | tf_op jit(solution)/shard_map/ppermute | solution.py:501
  89.7 3.3 %taps.1.part_ref = f32[256,1024]{1,0:T(8,128)} custom-call(bf16[512,256]{1,0:T(8,128)(2,1)} %get-tuple-element.33.high_ref, bf16[512,256]{1,0:T(8,128)(2,1)} %get-tuple-element.34.low_ref, f32[256,1024]{1,0:T(8,128)} %get-tuple-element.44.cube_ref), custom_call_target="tpu_custom_call" | custom-call | flops 805306368 | bytes 2097152 | tf_op jit(solution)/shard_map/taps/pallas_call | solution.py:421
  93.0 0.0 collective-permute-done.before_ref
  93.0 0.0 copy-start.2
  93.0 0.0 collective-permute-done.1.after_ref
  93.0 0.6 copy-done.2
  93.6 0.0 copy-start.3
  93.6 0.6 copy-done.3
  94.2 2.1 %edges.1 = f32[256,1024]{1,0:T(8,128)} custom-call(bf16[512,256]{1,0:T(8,128)(2,1)} %get-tuple-element.33.high_ref, bf16[512,256]{1,0:T(8,128)(2,1)} %get-tuple-element.34.low_ref, f32[16,256]{1,0:T(8,128)} %copy-done.2, f32[16,256]{1,0:T(8,128)} %copy-done.3, f32[256,1024]{1,0:T(8,128)} %taps.1.part_ref), custom_call_target="tpu_custom_call", output_to_operand_aliasing={{}: (4, {})} | custom-call | tf_op jit(solution)/shard_map/edges/pallas_call | solution.py:446
  (2 shorter events, 0.0 us)
Async XLA Ops:
  35.7 7.7 %copy-start = (f32[32,56,128]{2,1,0:T(8,128)}, f32[32,56,128]{2,1,0:T(8,128)S(1)}, u32[]{:S(2)}) copy-start(f32[32,56,128]{2,1,0:T(8,128)S(1)} %all_to_all.15) | copy-start | bytes 2752516
  35.7 30.9 %all-to-all-start.2 = ((f32[32,56,128]{2,1,0:T(8,128)}), f32[32,56,128]{2,1,0:T(8,128)S(1)}, u32[]{:S(2)}, u32[]{:S(2)}) async-start(f32[32,56,128]{2,1,0:T(8,128)} %get-tuple-element.38), calls=%async_computation.2 | async-start | bytes 1835008 | tf_op jit(solution)/shard_map/all_to_all | solution.py:479
  66.6 0.9 copy-start.1
  83.7 9.3 %collective-permute-start = (f32[16,256]{1,0:T(8,128)}, f32[16,256]{1,0:T(8,128)S(1)}, u32[]{:S(2)}, u32[]{:S(2)}) collective-permute-start(f32[16,256]{1,0:T(8,128)} %get-tuple-element.42), channel_id=1, source_target_pairs={{0,1},{1,2},{2,3},{4,5},{5,6},{6,7},{8,9},{9,10},{10,11},{12,13},{... | collective-permute-start | bytes 49160 | tf_op jit(solution)/shard_map/ppermute | solution.py:500
  87.7 5.3 %collective-permute-start.1 = (f32[16,256]{1,0:T(8,128)}, f32[16,256]{1,0:T(8,128)S(1)}, u32[]{:S(2)}, u32[]{:S(2)}) collective-permute-start(f32[16,256]{1,0:T(8,128)} %get-tuple-element.43), channel_id=1, source_target_pairs={{1,0},{2,1},{3,2},{5,4},{6,5},{7,6},{9,8},{10,9},{11,10},{13,12},{... | collective-permute-start | bytes 49160 | tf_op jit(solution)/shard_map/ppermute | solution.py:501
  93.0 0.6 copy-start.2
  93.6 0.6 copy-start.3
where the time goes:
time: 96.8 us; the launch traced here: 96.4 us
  Pallas kernels  53.5 us (55%)
  blocking collectives  27.3 us (28%)
  starting transfers between devices  12 us (12%)
  local copies, waits for them, and re-layouts  2.29 us (2%)
    all_to_all x1, blocking collectives, exchange(): lax.all_to_all(piece, ('tile', 'slab'), split_axis=0, concat_axis=0, tile...  27.3 us
    pallas_call x1, Pallas kernels, deposit_first(): pl.pallas_call(functools.partial(first_kernel, size, per_dest, share), ou...  21.8 us
    pallas_call x1, Pallas kernels, deposit_last(): pl.pallas_call(functools.partial(last_kernel, size, first, per_dest), out...  16.2 us
    pallas_call x1, Pallas kernels, pack(): pl.pallas_call(functools.partial(pack_kernel, sizes, slab_count, share),...  8.41 us
    all_to_all x1, starting transfers between devices, exchange(): lax.all_to_all(piece, ('tile', 'slab'), split_axis=0, concat_axis=0, tile...  6.02 us
    ppermute x1, starting transfers between devices, body(): before = lax.ppermute(tail, 'slab', [(i, i + 1) for i in range(ends)])  4.04 us
    pallas_call x1, Pallas kernels, sum_taps(): pl.pallas_call(taps_kernel, out_shape=jax.ShapeDtypeStruct(cube.shape, jn...  3.35 us
    pallas_call x1, Pallas kernels, add_edges(): pl.pallas_call(edge_kernel, out_shape=jax.ShapeDtypeStruct(part.shape, jn...  2.13 us
  transfers between devices with their start and end apart: 3, of which 0 were waited for; matrix products, arithmetic and copies ran while one was open for 1% of the time, Pallas kernels for 28%

commit v1 on v0

--- a/solution.py
+++ b/solution.py
@@ -18,6 +18,7 @@
 NCB = 32
 FIELDS = 6
 UNROLL = 6
+SKIP = 4
 LOG2E = math.log2(math.e)
 SMEM = pl.BlockSpec(memory_space=pltpu.SMEM)
 VMEM = pl.BlockSpec(memory_space=pltpu.VMEM)
@@ -25,8 +26,8 @@
 
 
 def chunk_sizes(per_dest):
-    part = max(per_dest * 3 // 8, 1)
-    sizes = [part, part, per_dest - 2 * part]
+    early = late = max(per_dest * 9 // 24, 1)
+    sizes = [early, late, per_dest - early - late]
     return [size for size in sizes if size > 0]
 
 
@@ -34,13 +35,47 @@
     return -(-rows // 8) * 8
 
 
-def pack_kernel(sizes, slab_count, share, slot_ref, count_ref, chan_ref, cell_ref, offset_ref, center_ref,
+def pack_kernel(sizes, wanted, slab_count, share, slot_ref, count_ref, chan_ref, cell_ref, offset_ref, center_ref,
                 width_ref, lum_ref, *refs):
-    outs, (props, stream) = refs[: len(sizes)], refs[len(sizes) :]
-    dest_count = outs[0].shape[0]
+    outs = dict(zip(wanted, refs))
+    props, stream, slots, counts, chans, plan, moves, sem = refs[len(wanted) :]
+    dest_count = slots.shape[0]
     per_dest = sum(sizes)
-    lane = lax.broadcasted_iota(jnp.int32, (8, ROWS), 1)
-    row_lane = lax.broadcasted_iota(jnp.int32, (1, ROWS), 1)
+    block_total = cell_ref.shape[0]
+    lane = lax.broadcasted_iota(jnp.int32, (dest_count, ROWS), 1)
+
+    slot_row = slot_ref[...]
+    blocks = lax.broadcasted_iota(jnp.int32, (block_total, slot_row.shape[1]), 0)
+    chosen = jnp.where(blocks == slot_row, 1.0, 0.0).astype(jnp.bfloat16)
+    table = jnp.concatenate([count_ref[...].reshape(1, -1), chan_ref[...].reshape(1, -1)], axis=0).astype(jnp.float32).astype(jnp.bfloat16)
+    looked = jnp.dot(table, chosen, preferred_element_type=jnp.float32)
+    slots[...] = jnp.zeros_like(slots)
+    counts[...] = jnp.zeros_like(counts)
+    chans[...] = jnp.zeros_like(chans)
+    for dest in range(dest_count):
+        columns = slice(dest * per_dest, (dest + 1) * per_dest)
+        slots[dest : dest + 1, :per_dest] = slot_row[:, columns]
+        counts[dest : dest + 1, :per_dest] = looked[0:1, columns]
+        chans[dest : dest + 1, :per_dest] = looked[1:2, columns]
+    count = counts[...]
+    until = jnp.dot(count.astype(jnp.bfloat16), exclusive(ROWS), preferred_element_type=jnp.float32)
+    end = until + count
+    start = until.astype(jnp.int32)
+    orders = jnp.zeros(lane.shape, jnp.int32)
+    for values in ((start >> 7) * 8, start & (ROWS - 1), jnp.maximum(slots[...], 0) * 8):
+        orders = jnp.where(lane < per_dest, values, pltpu.roll(orders, per_dest, 1))
+    plan[...] = orders
+    copy = pltpu.make_async_copy(plan, moves, sem)
+    copy.start()
+
+    if 0 in outs:
+        rows = outs[0].shape[0] // dest_count
+        dests = lax.broadcasted_iota(jnp.int32, lane.shape, 0)
+        chan = chans[...] - (lax.rem(dests, slab_count) * share).astype(jnp.float32)
+        longest = jnp.max(jnp.max(end, axis=0, keepdims=True), axis=1, keepdims=True)
+        meta = sizes[0] * FIELDS
+        outs[0][pl.ds(meta, dest_count, stride=rows), :] = jnp.where(lane == ROWS - 1, longest, chan)
+        outs[0][pl.ds(meta + 1, dest_count, stride=rows), :] = end
 
     def gather_fields(tile, carry):
         first = pl.multiple_of(tile * 8, 8)
@@ -57,62 +92,54 @@
             props[pl.ds(8 * first + field, 8, stride=8), :] = values
         return carry
 
-    lax.fori_loop(0, cell_ref.shape[0] // 8, gather_fields, 0, unroll=2)
-
-    def one_dest(dest, longest):
-        first_chan = lax.rem(dest, slab_count) * share
-        chan_row = jnp.zeros((1, ROWS), jnp.int32)
-        end_row = jnp.zeros((1, ROWS), jnp.int32)
-        start = jnp.int32(0)
+    lax.fori_loop(0, block_total // 8, gather_fields, 0, unroll=2)
+    copy.wait()
+    lanes = lax.broadcasted_iota(jnp.int32, (8, ROWS), 1)
+
+    def one_dest(dest, carry):
         for slot in range(per_dest):
-            block = slot_ref[0, dest * per_dest + slot]
-            filled = block >= 0
-            block = jnp.maximum(block, 0)
-            live = jnp.where(filled, count_ref[block], 0)
-            chan_row = jnp.where(row_lane == slot, chan_ref[block], chan_row)
-            shift = start & (ROWS - 1)
-            group = start >> 7
-            turned = pltpu.roll(props[pl.ds(pl.multiple_of(block * 8, 8), 8), :], shift, 1)
-            pltpu.store(stream.at[group], turned, mask=lane >= shift)
-            stream[group + 1] = turned
-            start = start + live
-            end_row = jnp.where(row_lane == slot, start, end_row)
+            row, shift, target = (moves[dest, k * per_dest + slot] for k in range(3))
+            row, target = pl.multiple_of(row, 8), pl.multiple_of(target, 8)
+            turned = pltpu.roll(props[pl.ds(row, 8), :], shift, 1)
+            pltpu.store(stream.at[pl.ds(target, 8), :], turned, mask=lanes >= shift)
+            stream[pl.ds(target + 8, 8), :] = turned
         group = 0
-        for out, size in zip(outs, sizes):
-            for place in range(size):
-                out[dest, place * FIELDS : (place + 1) * FIELDS, :] = stream[group, 0:FIELDS, :]
-                group += 1
-        meta = sizes[0] * FIELDS
-        outs[0][dest, meta : meta + 1, :] = (chan_row - first_chan).astype(jnp.float32)
-        outs[0][dest, meta + 1 : meta + 2, :] = end_row.astype(jnp.float32)
-        return jnp.maximum(longest, start)
-
-    longest = lax.fori_loop(0, dest_count, one_dest, jnp.int32(0))
-    meta = sizes[0] * FIELDS
-
-    def tell(dest, carry):
-        row = outs[0][dest, meta : meta + 1, :]
-        outs[0][dest, meta : meta + 1, :] = jnp.where(row_lane == ROWS - 1, longest.astype(jnp.float32), row)
+        for part, size in enumerate(sizes):
+            if part in outs:
+                out = outs[part]
+                base = pl.multiple_of(dest * (out.shape[0] // dest_count), 8)
+                for place in range(size):
+                    out[pl.ds(base + place * FIELDS, FIELDS), :] = stream[8 * (group + place) : 8 * (group + place) + FIELDS, :]
+            group += size
         return carry
 
-    lax.fori_loop(0, dest_count, tell, 0)
-
-
-def pack(sizes, dest_count, slab_count, share, slot_list, counts, chans, cells, offsets, centers, widths, lums):
-    rows = [size * FIELDS for size in sizes]
-    rows[0] += 2
+    lax.fori_loop(0, dest_count, one_dest, 0)
+
+
+def pack(sizes, wanted, dest_count, slab_count, share, slot_list, counts, chans, cells, offsets, centers, widths, lums):
+    rows = [padded_rows(size * FIELDS + (2 if part == 0 else 0)) for part, size in enumerate(sizes)]
     block_total = cells.shape[0]
-    return pl.pallas_call(
-        functools.partial(pack_kernel, sizes, slab_count, share),
-        out_shape=[jax.ShapeDtypeStruct((dest_count, padded_rows(r), ROWS), jnp.float32) for r in rows],
-        in_specs=[SMEM] * 3 + [VMEM] * 5,
-        out_specs=[VMEM] * len(sizes),
+    sent = pl.pallas_call(
+        functools.partial(pack_kernel, sizes, wanted, slab_count, share),
+        out_shape=[jax.ShapeDtypeStruct((dest_count * rows[part], ROWS), jnp.float32) for part in wanted],
+        in_specs=[VMEM] * 8,
+        out_specs=[VMEM] * len(wanted),
         scratch_shapes=[
             pltpu.VMEM((block_total * 8, ROWS), jnp.float32),
-            pltpu.VMEM((sum(sizes) + 2, 8, ROWS), jnp.float32),
+            pltpu.VMEM(((sum(sizes) + 2) * 8, ROWS), jnp.float32),
+            pltpu.VMEM((dest_count, ROWS), jnp.int32),
+            pltpu.VMEM((dest_count, ROWS), jnp.float32),
+            pltpu.VMEM((dest_count, ROWS), jnp.float32),
+            pltpu.VMEM((dest_count, ROWS), jnp.int32),
+            pltpu.SMEM((dest_count, ROWS), jnp.int32),
+            pltpu.SemaphoreType.DMA,
         ],
         name="pack",
-    )(slot_list, counts, chans, cells, offsets.reshape(block_total * 2, ROWS), centers, widths, lums)
+    )(
+        slot_list, counts, chans, cells,
+        offsets.reshape(block_total * 2, ROWS), centers, widths, lums,
+    )
+    return [piece.reshape(dest_count, rows[part], ROWS) for part, piece in zip(wanted, sent)]
 
 
 def exclusive(size):
@@ -141,6 +168,10 @@
         filled = filled + jnp.where(chan == float(c), here + above, 0.0)
         total = jnp.sum(jnp.sum(own, axis=0, keepdims=True), axis=1, keepdims=True)
         totals = totals + jnp.where(lane == c, total, 0.0)
+    for start in range(0, per_dest, SKIP):
+        inside = (lane >= start) & (lane < start + SKIP)
+        total = jnp.sum(jnp.where(inside, count, 0.0), axis=1, keepdims=True)
+        totals = totals + jnp.where(lane == share + start // SKIP, total, 0.0)
     filled = filled.astype(jnp.int32)
     begin = begin.astype(jnp.int32)
     base = lax.broadcasted_iota(jnp.int32, chan.shape, 0) * rows
@@ -161,8 +192,8 @@
     copy.start()
     copy.wait()
 
-    def append(source, carry):
-        for place in range(per_dest):
+    def move(source, places):
+        for place in places:
             row, begin, turn, target = (moves[source, k * per_dest + place] for k in range(4))
             target = pl.multiple_of(target, 8)
             here = got[pl.ds(row, FIELDS), :]
@@ -171,6 +202,14 @@
             whole = pltpu.roll(jnp.where(lane >= begin, here, there), turn, 1)
             pltpu.store(streams.at[pl.ds(target, FIELDS), :], whole, mask=lane >= filled)
             streams[pl.ds(target + 8, FIELDS), :] = whole
+
+    def append(source, carry):
+        if first == 0:
+            move(source, range(per_dest))
+        for start in range(0, 0 if first == 0 else per_dest, SKIP):
+            places = range(start, min(start + SKIP, per_dest))
+            live = moves[source, 4 * per_dest + share + start // SKIP]
+            pl.when(live > 0)(functools.partial(move, source, places))
         return carry
 
     lax.fori_loop(0, source_count, append, 0)
@@ -240,7 +279,7 @@
     return copy
 
 
-def first_kernel(size, per_dest, share, got_ref, acc, got, got_sem, *scratch):
+def first_kernel(size, per_dest, share, got_ref, acc, chan_ref, end_ref, got, got_sem, *scratch):
     copy = fetch(got_ref, got, got_sem)
     acc[...] = jnp.zeros_like(acc)
     sources = scratch[-2].shape[0]
@@ -248,6 +287,8 @@
     copy.wait()
     chan = got[pl.ds(size * FIELDS, sources, stride=rows), :]
     end = got[pl.ds(size * FIELDS + 1, sources, stride=rows), :]
+    chan_ref[...] = chan
+    end_ref[...] = end
     add_emitters(size, 0, per_dest, chan, end, got, acc, *scratch)
 
 
@@ -258,22 +299,24 @@
     add_emitters(size, first, per_dest, chan_ref[...], end_ref[...], got, acc, *scratch)
 
 
-def last_kernel(size, first, per_dest, chan_ref, end_ref, got_ref, held_ref, width_ref, cube_ref, head_ref, tail_ref,
-                acc, got, got_sem, *scratch):
+def last_kernel(size, first, per_dest, chan_ref, end_ref, width_ref, got_ref, held_ref, cube, head_ref, tail_ref,
+                acc, held_sem, got, got_sem, *scratch):
+    held = pltpu.make_async_copy(held_ref, acc, held_sem)
+    held.start()
     copy = fetch(got_ref, got, got_sem)
-    acc[...] = held_ref[...]
     copy.wait()
+    held.wait()
     add_emitters(size, first, per_dest, chan_ref[...], end_ref[...], got, acc, *scratch)
     share = acc.shape[0]
 
     def one_chan(chan, carry):
         columns = pl.ds(pl.multiple_of(chan * CB, CB), CB)
-        smooth(acc.at[chan], width_ref[:, columns], cube_ref, columns)
+        smooth(acc.at[chan], width_ref[:, columns], cube, columns)
         return carry
 
     lax.fori_loop(0, share, one_chan, 0)
-    head_ref[...] = cube_ref[:, :CB].T[:EDGE]
-    tail_ref[...] = cube_ref[:, (share - 1) * CB :].T[CB - EDGE :]
+    head_ref[...] = cube[:, :CB].T[:EDGE]
+    tail_ref[...] = cube[:, (share - 1) * CB :].T[CB - EDGE :]
 
 
 def smooth(plane_ref, widths, cube_ref, columns):
@@ -321,7 +364,7 @@
 
 
 def flat(got):
-    return got.reshape(-1, ROWS)
+    return pltpu.with_memory_space_constraint(got.reshape(-1, ROWS), pltpu.VMEM)
 
 
 def emitter_cost(size, got):
@@ -334,9 +377,10 @@
 def deposit_first(size, per_dest, share, got):
     return pl.pallas_call(
         functools.partial(first_kernel, size, per_dest, share),
-        out_shape=jax.ShapeDtypeStruct((share, PIX, CB), jnp.float32),
+        out_shape=[jax.ShapeDtypeStruct((share, PIX, CB), jnp.float32)]
+        + [jax.ShapeDtypeStruct((got.shape[0], ROWS), jnp.float32)] * 2,
         in_specs=[ANY],
-        out_specs=VMEM,
+        out_specs=[VMEM] * 3,
         scratch_shapes=emitter_scratch(size, got, share),
         cost_estimate=emitter_cost(size, got),
         name="deposit_first",
@@ -360,12 +404,16 @@
     return pl.pallas_call(
         functools.partial(last_kernel, size, first, per_dest),
         out_shape=[jax.ShapeDtypeStruct((PIX, share * CB), jnp.float32), edge, edge],
-        in_specs=[VMEM, VMEM, ANY, VMEM, VMEM],
+        in_specs=[VMEM] * 3 + [ANY] * 2,
         out_specs=[VMEM] * 3,
-        scratch_shapes=[pltpu.VMEM((share, PIX, CB), jnp.float32)] + emitter_scratch(size, got, share),
+        scratch_shapes=[
+            pltpu.VMEM((share, PIX, CB), jnp.float32),
+            pltpu.SemaphoreType.DMA,
+        ]
+        + emitter_scratch(size, got, share),
         cost_estimate=emitter_cost(size, got),
         name="deposit_last",
-    )(chan, end, flat(got), held, widths.reshape(1, -1))
+    )(chan, end, widths.reshape(1, -1), flat(got), held)
 
 
 def split(values):
@@ -382,76 +430,77 @@
     return dot(left_high, right_high) + (dot(left_high, right_low) + dot(left_low, right_high))
 
 
-def band_kernel(taps_ref, high_ref, low_ref):
-    rows, columns = high_ref.shape
-    apart = lax.broadcasted_iota(jnp.int32, (3 * CB, CB), 0) - lax.broadcasted_iota(jnp.int32, (3 * CB, CB), 1)
-    band = jnp.zeros((3 * CB, CB), jnp.float32)
+def band_part(taps_ref, first, rows):
+    shape = (rows, CB)
+    apart = lax.broadcasted_iota(jnp.int32, shape, 0) - lax.broadcasted_iota(jnp.int32, shape, 1) + (first + HALF)
+    band = jnp.zeros(shape, jnp.float32)
     for k in range(TAPS):
-        band = jnp.where(apart == CB - HALF + k, taps_ref[k], band)
-    high, low = split(band)
-    high_ref[...] = jnp.zeros_like(high_ref)
-    low_ref[...] = jnp.zeros_like(low_ref)
-    for i in range(columns // CB):
-        high_ref[i * CB : (i + 3) * CB, i * CB : (i + 1) * CB] = high
-        low_ref[i * CB : (i + 3) * CB, i * CB : (i + 1) * CB] = low
-
-
-def bands(taps, wide):
-    return pl.pallas_call(
-        band_kernel,
-        out_shape=[jax.ShapeDtypeStruct((wide + 2 * CB, wide), jnp.bfloat16)] * 2,
-        in_specs=[SMEM],
-        out_specs=[VMEM] * 2,
-        name="bands",
-    )(taps)
-
-
-def taps_kernel(high_ref, low_ref, cube_ref, out_ref):
-    wide = high_ref.shape[1]
-    end = cube_ref.shape[1]
+        band = jnp.where(apart == k, taps_ref[k], band)
+    return split(band)
+
+
+def taps_kernel(wide, taps_ref, cube_ref, out_ref, cube, high_ref, low_ref, sem):
+    copy = pltpu.make_async_copy(cube_ref, cube, sem)
+    copy.start()
+    for ref, part in zip((high_ref, low_ref), band_part(taps_ref, -CB, 3 * CB)):
+        ref[...] = jnp.zeros_like(ref)
+        for i in range(0, wide, CB):
+            ref[i : i + 3 * CB, i : i + CB] = part
+    copy.wait()
+    end = cube.shape[1]
     for start in range(0, end, wide):
         low, high = max(start - CB, 0), min(start + wide + CB, end)
         rows = slice(low - start + CB, high - start + CB)
         out_ref[:, start : start + wide] = times(
-            split(cube_ref[:, low:high]), (high_ref[rows], low_ref[rows]), ((1,), (0,))
+            split(cube[:, low:high]), (high_ref[rows], low_ref[rows]), ((1,), (0,))
         )
 
 
-def sum_taps(band, cube):
+def sum_taps(taps, cube):
+    wide = 2 * CB if cube.shape[1] % (2 * CB) == 0 else CB
     return pl.pallas_call(
-        taps_kernel,
+        functools.partial(taps_kernel, wide),
         out_shape=jax.ShapeDtypeStruct(cube.shape, jnp.float32),
-        in_specs=[VMEM] * 3,
+        in_specs=[SMEM, ANY],
         out_specs=VMEM,
+        scratch_shapes=[pltpu.VMEM(cube.shape, jnp.float32)]
+        + [pltpu.VMEM((wide + 2 * CB, wide), jnp.bfloat16)] * 2
+        + [pltpu.SemaphoreType.DMA],
         cost_estimate=pl.CostEstimate(
-            flops=6 * cube.size * band[0].shape[0], transcendentals=0, bytes_accessed=cube.size * 8
+            flops=6 * cube.size * (wide + 2 * CB), transcendentals=0, bytes_accessed=cube.size * 8
         ),
         name="taps",
-    )(*band, cube)
-
-
-def edge_kernel(high_ref, low_ref, before_ref, after_ref, part_ref, out_ref):
+    )(taps, cube)
+
+
+def edge_kernel(taps_ref, before_ref, after_ref, part_ref, out_ref):
     side = pl.program_id(0)
-    edge = jnp.where(side == 0, before_ref[...], after_ref[...])
-    out_ref[...] = part_ref[...] + times(split(edge), (high_ref[...], low_ref[...]), ((0,), (0,)))
-
-
-def add_edges(band, before, after, part):
+    slab, last = lax.axis_index("slab"), lax.axis_size("slab") - 1
+
+    @pl.when(side == 0)
+    def _():
+        edge = jnp.where(slab > 0, before_ref[...], 0.0)
+        out_ref[...] = part_ref[...] + times(split(edge), band_part(taps_ref, -EDGE, EDGE), ((0,), (0,)))
+
+    @pl.when(side == 1)
+    def _():
+        edge = jnp.where(slab < last, after_ref[...], 0.0)
+        out_ref[...] = part_ref[...] + times(split(edge), band_part(taps_ref, CB, EDGE), ((0,), (0,)))
+
+
+def add_edges(taps, before, after, part):
     last = part.shape[1] // CB - 1
-    rows, columns = band[0].shape
-    top, bottom = (CB - EDGE) // EDGE, (rows - CB) // EDGE
-    corner = pl.BlockSpec((EDGE, CB), lambda i: (top + i * (bottom - top), i * (columns // CB - 1)))
-    edge = pl.BlockSpec((EDGE, PIX), lambda i: (0, 0))
     block = pl.BlockSpec((PIX, CB), lambda i: (0, i * last))
+    before, after = (pltpu.with_memory_space_constraint(e, pltpu.VMEM) for e in (before, after))
     return pl.pallas_call(
         edge_kernel,
         out_shape=jax.ShapeDtypeStruct(part.shape, jnp.float32),
         grid=(2,),
-        in_specs=[corner, corner, edge, edge, block],
+        in_specs=[SMEM, VMEM, VMEM, block],
         out_specs=block,
-        input_output_aliases={4: 0},
+        input_output_aliases={3: 0},
         name="edges",
-    )(*band, before, after, part)
+    )(taps, before, after, part)
 
 
 def body(
@@ -471,35 +520,37 @@
     per_dest = slot_table.shape[1] // dest_count
     share = NCB // slab_count
     sizes = chunk_sizes(per_dest)
-    sent = pack(
-        sizes, dest_count, slab_count, share, slot_table, block_rows, block_chan,
-        voxel_cell, offsets, line_center, line_width, luminosity,
-    )
+
+    def packed(wanted):
+        return pack(
+            sizes, wanted, dest_count, slab_count, share, slot_table, block_rows, block_chan,
+            voxel_cell, offsets, line_center, line_width, luminosity,
+        )
+
+    sent = packed((0, 1))
     def exchange(piece):
         return lax.all_to_all(piece, ("tile", "slab"), split_axis=0, concat_axis=0, tiled=True)
 
     got_first = exchange(sent[0])
     got_first, last_piece = lax.optimization_barrier((got_first, sent[1]))
     got_last = exchange(last_piece)
-    chan = got_first[:, sizes[0] * FIELDS, :]
-    end = got_first[:, sizes[0] * FIELDS + 1, :]
-    band = bands(spectral_taps, 2 * CB if share % 2 == 0 else CB)
-    held = deposit_first(sizes[0], per_dest, share, got_first)
+    held, chan, end = deposit_first(sizes[0], per_dest, share, got_first)
     reach = sizes[0] + sizes[1]
     if len(sizes) > 2:
         longest = jnp.max(chan[:, ROWS - 1])
         held, got_last = lax.optimization_barrier((held, got_last))
         held = lax.cond(
             longest > float(reach * ROWS),
-            lambda held: deposit_more(sizes[2], reach, per_dest, share, chan, end, exchange(sent[2]), held),
+            lambda held: deposit_more(sizes[2], reach, per_dest, share, chan, end, exchange(packed((2,))[0]), held),
             lambda held: held,
             held,
         )
-    cube, head, tail = deposit_last(sizes[1], sizes[0], per_dest, share, chan, end, got_last, held, beam_width)
-    ends = slab_count - 1
-    before = lax.ppermute(tail, "slab", [(i, i + 1) for i in range(ends)])
-    after = lax.ppermute(head, "slab", [(i + 1, i) for i in range(ends)])
-    return add_edges(band, before, after, sum_taps(band, cube))[None]
+    cube, head, tail = deposit_last(
+        sizes[1], sizes[0], per_dest, share, chan, end, got_last, held, beam_width
+    )
+    before = lax.ppermute(tail, "slab", [(i, (i + 1) % slab_count) for i in range(slab_count)])
+    after = lax.ppermute(head, "slab", [((i + 1) % slab_count, i) for i in range(slab_count)])
+    return add_edges(spectral_taps, before, after, sum_taps(spectral_taps, cube))[None]
 
 
 def solution(mesh):

time: 96.8 us -> 90.2 us (0.932)
  the two profiles are of different devices: /device:TPU:13 before, /device:TPU:1 now
where the time goes in v1:
time: 90.2 us; the launch traced here: 89.3 us
  Pallas kernels  35.7 us (40%)
  blocking collectives  29.7 us (33%)
  starting transfers between devices  15.3 us (17%)
  waiting for transfers between devices  7.14 us (8%)
    all_to_all x1, blocking collectives, exchange(): lax.all_to_all(piece, ('tile', 'slab'), split_axis=0, concat_axis=0, tile...  29.7 us
    pallas_call x1, Pallas kernels, deposit_first(): pl.pallas_call(functools.partial(first_kernel, size, per_dest, share), ou...  14.1 us
    ppermute x1, starting transfers between devices, body(): lax.ppermute(tail, 'slab', [(i, (i + 1) % slab_count) for i in range(slab...  10.9 us
    pallas_call x1, Pallas kernels, deposit_last(): pl.pallas_call(functools.partial(last_kernel, size, first, per_dest), out...  8.02 us
    pallas_call x1, Pallas kernels, pack(): pl.pallas_call(functools.partial(pack_kernel, sizes, wanted, slab_count,...  7.55 us
    all_to_all x1, waiting for transfers between devices, exchange(): lax.all_to_all(piece, ('tile', 'slab'), split_axis=0, concat_axis=0, tile...  7.13 us
    all_to_all x1, starting transfers between devices, exchange(): lax.all_to_all(piece, ('tile', 'slab'), split_axis=0, concat_axis=0, tile...  4.39 us
    pallas_call x1, Pallas kernels, sum_taps(): pl.pallas_call(functools.partial(taps_kernel, wide), out_shape=jax.ShapeD...  3.85 us
  transfers between devices with their start and end apart: 3, of which 1 were waited for; matrix products, arithmetic and copies ran while one was open for 1% of the time, Pallas kernels for 20%

profile of v1, /device:TPU:1, one launch (start us, length us, event | category | flops | bytes accessed | tf_op | source)
XLA Modules:
  0.0 89.3 jit_solution(17779812101390422564)
XLA Ops:
  0.0 7.5 %pack.3 = (f32[1792,128]{1,0:T(8,128)}, f32[1792,128]{1,0:T(8,128)}) custom-call(s32[1,768]{1,0:T(1,128)} %slot_ref.1, s32[384]{0:T(512)} %count_ref.1, s32[384]{0:T(512)} %chan_ref.1, s32[384,128]{1,0:T(8,128)} %cell_ref.1, f32[768,128]{1,0:T(8,128)} %bitcast.14, f32[384,128]{1,0:T(8,128)} %center_ref.1, f32[384,128]{1,0:T(8,128)} %width_ref.1, ...), custom_call_target="tpu_custom_call" | custom-call | tf_op jit(solution)/shard_map/pack/pallas_call | solution.py:122
  7.6 29.7 %all_to_all.15 = f32[32,56,128]{2,1,0:T(8,128)S(1)} all-to-all(f32[32,56,128]{2,1,0:T(8,128)} %bitcast.16), channel_id=1, replica_groups=mesh['tile'=8,'slab'=4] {'tile','slab'}, dimensions={0} | all-to-all | bytes 1835008 | tf_op jit(solution)/shard_map/all_to_all | solution.py:532
  37.3 4.4 %all-to-all-start.2 = ((f32[32,56,128]{2,1,0:T(8,128)}), f32[32,56,128]{2,1,0:T(8,128)S(1)}, u32[]{:S(2)}, u32[]{:S(2)}) async-start(f32[32,56,128]{2,1,0:T(8,128)} %bitcast.5), calls=%async_computation.2 | async-start | bytes 1835008 | tf_op jit(solution)/shard_map/all_to_all | solution.py:532
  41.7 0.0 copy-start
  41.7 0.0 copy-start.1
  41.7 0.0 copy-start.4
  41.7 14.1 %deposit_first.1 = (f32[8,256,128]{2,1,0:T(8,128)S(1)}, f32[32,128]{1,0:T(8,128)S(1)}, f32[32,128]{1,0:T(8,128)S(1)}) custom-call(f32[1792,128]{1,0:T(8,128)S(1)} %bitcast.12), custom_call_target="tpu_custom_call" | custom-call | flops 2415919104 | bytes 917504 | tf_op jit(solution)/shard_map/deposit_first/pallas_call | solution.py:378
  55.8 0.7 slice_reduce_fusion
  57.2 0.0 copy-start.2
  57.2 0.0 copy-start.3
  57.2 7.1 %all-to-all-done.2 = f32[32,56,128]{2,1,0:T(8,128)S(1)} async-done(((f32[32,56,128]{2,1,0:T(8,128)}), f32[32,56,128]{2,1,0:T(8,128)S(1)}, u32[]{:S(2)}, u32[]{:S(2)}) %all-to-all-start.2) | async-done | bytes 917536 | tf_op jit(solution)/shard_map/all_to_all | solution.py:532
  64.3 0.0 copy-done
  64.3 0.0 copy-done.1
  64.3 0.0 copy-done.4
  64.3 0.0 copy-done.2
  64.3 0.0 copy-done.3
  64.4 8.0 %deposit_last.1 = (f32[256,1024]{1,0:T(8,128)}, f32[16,256]{1,0:T(8,128)}, f32[16,256]{1,0:T(8,128)}) custom-call(f32[32,128]{1,0:T(8,128)S(1)} %get-tuple-element.57.chan_ref, f32[32,128]{1,0:T(8,128)S(1)} %get-tuple-element.58.end_ref, f32[1,1024]{1,0:T(1,128)} %bitcast.17, f32[1792,128]{1,0:T(8,128)S(1)} %bitcast.11, ...), custom_call_target="tpu_custom_call" | custom-call | flops 2415919104 | bytes 917504 | tf_op jit(solution)/shard_map/deposit_last/pallas_call | solution.py:404
  72.4 10.9 %collective-permute-start = (f32[16,256]{1,0:T(8,128)}, f32[16,256]{1,0:T(8,128)S(1)}, u32[]{:S(2)}, u32[]{:S(2)}) collective-permute-start(f32[16,256]{1,0:T(8,128)} %get-tuple-element.63), channel_id=1, source_target_pairs={{0,1},{1,2},{2,3},{3,0},{4,5},{5,6},{6,7},{7,4},{8,9},{9,10},{10,1... | collective-permute-start | bytes 49160 | tf_op jit(solution)/shard_map/ppermute | solution.py:551
  83.3 0.0 collective-permute-start.1
  83.3 3.8 %taps.1.part_ref = f32[256,1024]{1,0:T(8,128)} custom-call(f32[31]{0:T(128)} %taps_ref.3, f32[256,1024]{1,0:T(8,128)} %get-tuple-element.65.cube_ref), custom_call_target="tpu_custom_call" | custom-call | flops 805306368 | bytes 2097152 | tf_op jit(solution)/shard_map/taps/pallas_call | solution.py:461
  87.1 0.0 collective-permute-done.before_ref
  87.1 0.0 collective-permute-done.1.after_ref
  87.1 2.1 %edges.1 = f32[256,1024]{1,0:T(8,128)} custom-call(f32[31]{0:T(128)} %taps_ref.3, f32[16,256]{1,0:T(8,128)S(1)} %collective-permute-done.before_ref, f32[16,256]{1,0:T(8,128)S(1)} %collective-permute-done.1.after_ref, f32[256,1024]{1,0:T(8,128)} %taps.1.part_ref), custom_call_target="tpu_custom_call", output_to_operand_aliasing={{}: (3, {})} | custom-call | tf_op jit(solution)/shard_map/edges/pallas_call | solution.py:495
  (1 shorter events, 0.0 us)
Async XLA Ops:
  37.3 27.0 %all-to-all-start.2 = ((f32[32,56,128]{2,1,0:T(8,128)}), f32[32,56,128]{2,1,0:T(8,128)S(1)}, u32[]{:S(2)}, u32[]{:S(2)}) async-start(f32[32,56,128]{2,1,0:T(8,128)} %bitcast.5), calls=%async_computation.2 | async-start | bytes 1835008 | tf_op jit(solution)/shard_map/all_to_all | solution.py:532
  41.7 22.6 %copy-start = (f32[384,2,128]{2,1,0:T(2,128)S(1)}, f32[384,2,128]{2,1,0:T(2,128)}, u32[]{:S(2)}) copy-start(f32[384,2,128]{2,1,0:T(2,128)} %param.13) | copy-start | bytes 1179652
  41.7 22.6 %copy-start.1 = (s32[384,128]{1,0:T(8,128)S(1)}, s32[384,128]{1,0:T(8,128)}, u32[]{:S(2)}) copy-start(s32[384,128]{1,0:T(8,128)} %cell_ref.1) | copy-start | bytes 589828
  41.7 22.6 %copy-start.4 = (s32[384]{0:T(512)S(1)}, s32[384]{0:T(512)}, u32[]{:S(2)}) copy-start(s32[384]{0:T(512)} %chan_ref.1) | copy-start | bytes 4612
  57.2 7.2 %copy-start.2 = (s32[1,768]{1,0:T(1,128)S(1)}, s32[1,768]{1,0:T(1,128)}, u32[]{:S(2)}) copy-start(s32[1,768]{1,0:T(1,128)} %slot_ref.1) | copy-start | bytes 9220
  57.2 7.2 %copy-start.3 = (s32[384]{0:T(512)S(1)}, s32[384]{0:T(512)}, u32[]{:S(2)}) copy-start(s32[384]{0:T(512)} %count_ref.1) | copy-start | bytes 4612
  72.4 14.7 %collective-permute-start = (f32[16,256]{1,0:T(8,128)}, f32[16,256]{1,0:T(8,128)S(1)}, u32[]{:S(2)}, u32[]{:S(2)}) collective-permute-start(f32[16,256]{1,0:T(8,128)} %get-tuple-element.63), channel_id=1, source_target_pairs={{0,1},{1,2},{2,3},{3,0},{4,5},{5,6},{6,7},{7,4},{8,9},{9,10},{10,1... | collective-permute-start | bytes 49160 | tf_op jit(solution)/shard_map/ppermute | solution.py:551
  83.3 3.9 %collective-permute-start.1 = (f32[16,256]{1,0:T(8,128)}, f32[16,256]{1,0:T(8,128)S(1)}, u32[]{:S(2)}, u32[]{:S(2)}) collective-permute-start(f32[16,256]{1,0:T(8,128)} %get-tuple-element.64), channel_id=1, source_target_pairs={{1,0},{2,1},{3,2},{0,3},{5,4},{6,5},{7,6},{4,7},{9,8},{10,9},{11,1... | collective-permute-start | bytes 49160 | tf_op jit(solution)/shard_map/ppermute | solution.py:552

commit v2 on v1

--- a/solution.py
+++ b/solution.py
@@ -18,7 +18,7 @@
 NCB = 32
 FIELDS = 6
 UNROLL = 6
-SKIP = 4
+SKIP = 8
 LOG2E = math.log2(math.e)
 SMEM = pl.BlockSpec(memory_space=pltpu.SMEM)
 VMEM = pl.BlockSpec(memory_space=pltpu.VMEM)
@@ -182,7 +182,7 @@
     plan[...] = table
 
 
-def add_emitters(size, first, per_dest, chan, end, got, acc, streams, todo, plan, moves, sem):
+def add_emitters(size, first, per_dest, chan, end, got, acc, streams, todo, plan, moves, sem, ready=()):
     source_count = chan.shape[0]
     share = acc.shape[0]
     stride = streams.shape[0] // (8 * share)
@@ -191,6 +191,8 @@
     copy = pltpu.make_async_copy(plan, moves, sem)
     copy.start()
     copy.wait()
+    for other in ready:
+        other.wait()
 
     def move(source, places):
         for place in places:
@@ -299,14 +301,12 @@
     add_emitters(size, first, per_dest, chan_ref[...], end_ref[...], got, acc, *scratch)
 
 
-def last_kernel(size, first, per_dest, chan_ref, end_ref, width_ref, got_ref, held_ref, cube, head_ref, tail_ref,
+def last_kernel(size, first, per_dest, chan_ref, end_ref, width_ref, got_ref, held_ref, cube, near_ref, far_ref,
                 acc, held_sem, got, got_sem, *scratch):
     held = pltpu.make_async_copy(held_ref, acc, held_sem)
     held.start()
     copy = fetch(got_ref, got, got_sem)
-    copy.wait()
-    held.wait()
-    add_emitters(size, first, per_dest, chan_ref[...], end_ref[...], got, acc, *scratch)
+    add_emitters(size, first, per_dest, chan_ref[...], end_ref[...], got, acc, *scratch, ready=(copy, held))
     share = acc.shape[0]
 
     def one_chan(chan, carry):
@@ -315,8 +315,11 @@
         return carry
 
     lax.fori_loop(0, share, one_chan, 0)
-    head_ref[...] = cube[:, :CB].T[:EDGE]
-    tail_ref[...] = cube[:, (share - 1) * CB :].T[CB - EDGE :]
+    even = lax.rem(lax.axis_index("slab"), 2) == 0
+    head = cube[:, :CB].T[:EDGE]
+    tail = cube[:, (share - 1) * CB :].T[CB - EDGE :]
+    near_ref[...] = jnp.where(even, tail, head)
+    far_ref[...] = jnp.where(even, head, tail)
 
 
 def smooth(plane_ref, widths, cube_ref, columns):
@@ -439,68 +442,47 @@
     return split(band)
 
 
-def taps_kernel(wide, taps_ref, cube_ref, out_ref, cube, high_ref, low_ref, sem):
-    copy = pltpu.make_async_copy(cube_ref, cube, sem)
-    copy.start()
+def taps_kernel(wide, taps_ref, cube_hbm, near_ref, far_ref, out_ref, cube_ref, out, high_ref, low_ref, sem, sems):
+    fetched = pltpu.make_async_copy(cube_hbm, cube_ref, sem)
+    fetched.start()
+    slab, last = lax.axis_index("slab"), lax.axis_size("slab") - 1
+    even = lax.rem(slab, 2) == 0
     for ref, part in zip((high_ref, low_ref), band_part(taps_ref, -CB, 3 * CB)):
         ref[...] = jnp.zeros_like(ref)
         for i in range(0, wide, CB):
             ref[i : i + 3 * CB, i : i + CB] = part
-    copy.wait()
-    end = cube.shape[1]
+    end = cube_ref.shape[1]
+    copies = []
+    fetched.wait()
     for start in range(0, end, wide):
         low, high = max(start - CB, 0), min(start + wide + CB, end)
-        rows = slice(low - start + CB, high - start + CB)
-        out_ref[:, start : start + wide] = times(
-            split(cube[:, low:high]), (high_ref[rows], low_ref[rows]), ((1,), (0,))
-        )
-
-
-def sum_taps(taps, cube):
+        rows, columns = slice(low - start + CB, high - start + CB), slice(start, start + wide)
+        out[:, columns] = times(split(cube_ref[:, low:high]), (high_ref[rows], low_ref[rows]), ((1,), (0,)))
+        if start == 0:
+            edge = jnp.where(slab > 0, jnp.where(even, far_ref[...], near_ref[...]), 0.0)
+            out[:, :CB] += times(split(edge), band_part(taps_ref, -EDGE, EDGE), ((0,), (0,)))
+        if start + wide == end:
+            edge = jnp.where(slab < last, jnp.where(even, near_ref[...], far_ref[...]), 0.0)
+            out[:, end - CB :] += times(split(edge), band_part(taps_ref, CB, EDGE), ((0,), (0,)))
+        copies.append(pltpu.make_async_copy(out.at[:, columns], out_ref.at[:, columns], sems.at[start // wide]))
+        copies[-1].start()
+    for copy in copies:
+        copy.wait()
+
+
+def sum_taps(taps, cube, near, far):
     wide = 2 * CB if cube.shape[1] % (2 * CB) == 0 else CB
+    near, far = (pltpu.with_memory_space_constraint(x, pltpu.VMEM) for x in (near, far))
     return pl.pallas_call(
         functools.partial(taps_kernel, wide),
         out_shape=jax.ShapeDtypeStruct(cube.shape, jnp.float32),
-        in_specs=[SMEM, ANY],
-        out_specs=VMEM,
-        scratch_shapes=[pltpu.VMEM(cube.shape, jnp.float32)]
+        in_specs=[SMEM, ANY, VMEM, VMEM],
+        out_specs=ANY,
+        scratch_shapes=[pltpu.VMEM(cube.shape, jnp.float32)] * 2
         + [pltpu.VMEM((wide + 2 * CB, wide), jnp.bfloat16)] * 2
-        + [pltpu.SemaphoreType.DMA],
-        cost_estimate=pl.CostEstimate(
-            flops=6 * cube.size * (wide + 2 * CB), transcendentals=0, bytes_accessed=cube.size * 8
-        ),
+        + [pltpu.SemaphoreType.DMA, pltpu.SemaphoreType.DMA((cube.shape[1] // wide,))],
         name="taps",
-    )(taps, cube)
-
-
-def edge_kernel(taps_ref, before_ref, after_ref, part_ref, out_ref):
-    side = pl.program_id(0)
-    slab, last = lax.axis_index("slab"), lax.axis_size("slab") - 1
-
-    @pl.when(side == 0)
-    def _():
-        edge = jnp.where(slab > 0, before_ref[...], 0.0)
-        out_ref[...] = part_ref[...] + times(split(edge), band_part(taps_ref, -EDGE, EDGE), ((0,), (0,)))
-
-    @pl.when(side == 1)
-    def _():
-        edge = jnp.where(slab < last, after_ref[...], 0.0)
-        out_ref[...] = part_ref[...] + times(split(edge), band_part(taps_ref, CB, EDGE), ((0,), (0,)))
-
-
-def add_edges(taps, before, after, part):
-    last = part.shape[1] // CB - 1
-    block = pl.BlockSpec((PIX, CB), lambda i: (0, i * last))
-    before, after = (pltpu.with_memory_space_constraint(e, pltpu.VMEM) for e in (before, after))
-    return pl.pallas_call(
-        edge_kernel,
-        out_shape=jax.ShapeDtypeStruct(part.shape, jnp.float32),
-        grid=(2,),
-        in_specs=[SMEM, VMEM, VMEM, block],
-        out_specs=block,
-        input_output_aliases={3: 0},
-        name="edges",
-    )(taps, before, after, part)
+    )(taps, cube, near, far)
 
 
 def body(
@@ -545,12 +527,12 @@
             lambda held: held,
             held,
         )
-    cube, head, tail = deposit_last(
+    cube, near, far = deposit_last(
         sizes[1], sizes[0], per_dest, share, chan, end, got_last, held, beam_width
     )
-    before = lax.ppermute(tail, "slab", [(i, (i + 1) % slab_count) for i in range(slab_count)])
-    after = lax.ppermute(head, "slab", [((i + 1) % slab_count, i) for i in range(slab_count)])
-    return add_edges(spectral_taps, before, after, sum_taps(spectral_taps, cube))[None]
+    near = lax.ppermute(near, "slab", [(i, i ^ 1) for i in range(slab_count)])
+    far = lax.ppermute(far, "slab", [(i, (i + 1 if i % 2 else i - 1) % slab_count) for i in range(slab_count)])
+    return sum_taps(spectral_taps, cube, near, far)[None]
 
 
 def solution(mesh):

time: 90.2 us -> 87.7 us (0.972)
  the two profiles are of different devices: /device:TPU:1 before, /device:TPU:17 now
where the time goes in v2:
time: 87.7 us; the launch traced here: 86.4 us
  Pallas kernels  29.5 us (34%)
  blocking collectives  28.5 us (32%)
  starting transfers between devices  15.6 us (18%)
  waiting for transfers between devices  11.4 us (13%)
    all_to_all x1, blocking collectives, exchange(): lax.all_to_all(piece, ('tile', 'slab'), split_axis=0, concat_axis=0, tile...  28.5 us
    pallas_call x1, Pallas kernels, deposit_first(): pl.pallas_call(functools.partial(first_kernel, size, per_dest, share), ou...  11 us
    ppermute x1, starting transfers between devices, body(): lax.ppermute(far, 'slab', [(i, (i + 1 if i % 2 else i - 1) % slab_count)...  10.7 us
    all_to_all x1, waiting for transfers between devices, exchange(): lax.all_to_all(piece, ('tile', 'slab'), split_axis=0, concat_axis=0, tile...  9.8 us
    pallas_call x1, Pallas kernels, pack(): pl.pallas_call(functools.partial(pack_kernel, sizes, wanted, slab_count,...  7.55 us
    pallas_call x1, Pallas kernels, deposit_last(): pl.pallas_call(functools.partial(last_kernel, size, first, per_dest), out...  7.17 us
    all_to_all x1, starting transfers between devices, exchange(): lax.all_to_all(piece, ('tile', 'slab'), split_axis=0, concat_axis=0, tile...  4.8 us
    pallas_call x1, Pallas kernels, sum_taps(): pl.pallas_call(functools.partial(taps_kernel, wide), out_shape=jax.ShapeD...  3.75 us
  transfers between devices with their start and end apart: 3, of which 2 were waited for; matrix products, arithmetic and copies ran while one was open for 1% of the time, Pallas kernels for 13%

profile of v2, /device:TPU:17, one launch (start us, length us, event | category | flops | bytes accessed | tf_op | source)
XLA Modules:
  0.0 86.4 jit_solution(5579220349377518117)
XLA Ops:
  0.0 7.6 %pack.3 = (f32[1792,128]{1,0:T(8,128)}, f32[1792,128]{1,0:T(8,128)}) custom-call(s32[1,768]{1,0:T(1,128)} %slot_ref.1, s32[384]{0:T(512)} %count_ref.1, s32[384]{0:T(512)} %chan_ref.1, s32[384,128]{1,0:T(8,128)} %cell_ref.1, f32[768,128]{1,0:T(8,128)} %bitcast.14, f32[384,128]{1,0:T(8,128)} %center_ref.1, f32[384,128]{1,0:T(8,128)} %width_ref.1, ...), custom_call_target="tpu_custom_call" | custom-call | tf_op jit(solution)/shard_map/pack/pallas_call | solution.py:122
  7.6 28.5 %all_to_all.15 = f32[32,56,128]{2,1,0:T(8,128)S(1)} all-to-all(f32[32,56,128]{2,1,0:T(8,128)} %bitcast.16), channel_id=1, replica_groups=mesh['tile'=8,'slab'=4] {'tile','slab'}, dimensions={0} | all-to-all | bytes 1835008 | tf_op jit(solution)/shard_map/all_to_all | solution.py:514
  36.0 4.8 %all-to-all-start.2 = ((f32[32,56,128]{2,1,0:T(8,128)}), f32[32,56,128]{2,1,0:T(8,128)S(1)}, u32[]{:S(2)}, u32[]{:S(2)}) async-start(f32[32,56,128]{2,1,0:T(8,128)} %bitcast.5), calls=%async_computation.2 | async-start | bytes 1835008 | tf_op jit(solution)/shard_map/all_to_all | solution.py:514
  40.8 0.0 copy-start
  40.8 0.0 copy-start.1
  40.8 0.0 copy-start.4
  40.9 11.0 %deposit_first.1 = (f32[8,256,128]{2,1,0:T(8,128)S(1)}, f32[32,128]{1,0:T(8,128)S(1)}, f32[32,128]{1,0:T(8,128)S(1)}) custom-call(f32[1792,128]{1,0:T(8,128)S(1)} %bitcast.12), custom_call_target="tpu_custom_call" | custom-call | flops 2415919104 | bytes 917504 | tf_op jit(solution)/shard_map/deposit_first/pallas_call | solution.py:381
  51.9 0.7 slice_reduce_fusion
  53.2 0.0 copy-start.2
  53.2 0.0 copy-start.3
  53.2 9.8 %all-to-all-done.2 = f32[32,56,128]{2,1,0:T(8,128)S(1)} async-done(((f32[32,56,128]{2,1,0:T(8,128)}), f32[32,56,128]{2,1,0:T(8,128)S(1)}, u32[]{:S(2)}, u32[]{:S(2)}) %all-to-all-start.2) | async-done | bytes 917536 | tf_op jit(solution)/shard_map/all_to_all | solution.py:514
  63.0 0.0 copy-done
  63.0 0.0 copy-done.1
  63.0 0.0 copy-done.4
  63.0 0.0 copy-done.2
  63.1 0.0 copy-done.3
  63.1 7.2 %deposit_last.1 = (f32[256,1024]{1,0:T(8,128)}, f32[16,256]{1,0:T(8,128)}, f32[16,256]{1,0:T(8,128)}) custom-call(f32[32,128]{1,0:T(8,128)S(1)} %get-tuple-element.57.chan_ref, f32[32,128]{1,0:T(8,128)S(1)} %get-tuple-element.58.end_ref, f32[1,1024]{1,0:T(1,128)} %bitcast.17, f32[1792,128]{1,0:T(8,128)S(1)} %bitcast.11, ...), custom_call_target="tpu_custom_call" | custom-call | flops 2415919104 | bytes 917504 | tf_op jit(solution)/shard_map/deposit_last/pallas_call | solution.py:407
  70.3 0.1 collective-permute-start
  70.3 10.7 %collective-permute-start.1 = (f32[16,256]{1,0:T(8,128)}, f32[16,256]{1,0:T(8,128)S(1)}, u32[]{:S(2)}, u32[]{:S(2)}) collective-permute-start(f32[16,256]{1,0:T(8,128)} %get-tuple-element.65), channel_id=1, source_target_pairs={{0,3},{1,2},{2,1},{3,0},{4,7},{5,6},{6,5},{7,4},{8,11},{9,10},{10,... | collective-permute-start | bytes 49160 | tf_op jit(solution)/shard_map/ppermute | solution.py:534
  81.0 0.0 collective-permute-done.near_ref
  81.0 1.6 %collective-permute-done.1.far_ref = f32[16,256]{1,0:T(8,128)S(1)} collective-permute-done((f32[16,256]{1,0:T(8,128)}, f32[16,256]{1,0:T(8,128)S(1)}, u32[]{:S(2)}, u32[]{:S(2)}) %collective-permute-start.1) | collective-permute-done | bytes 16416 | tf_op jit(solution)/shard_map/ppermute | solution.py:534
  82.7 3.8 %taps.1 = f32[256,1024]{1,0:T(8,128)} custom-call(f32[31]{0:T(128)} %taps_ref.1, f32[256,1024]{1,0:T(8,128)} %get-tuple-element.63.cube_hbm, f32[16,256]{1,0:T(8,128)S(1)} %collective-permute-done.near_ref, f32[16,256]{1,0:T(8,128)S(1)} %collective-permute-done.1.far_ref), custom_call_target="tpu_custom_call" | custom-call | tf_op jit(solution)/shard_map/taps/pallas_call | solution.py:476
  (1 shorter events, 0.0 us)
Async XLA Ops:
  36.0 27.0 %all-to-all-start.2 = ((f32[32,56,128]{2,1,0:T(8,128)}), f32[32,56,128]{2,1,0:T(8,128)S(1)}, u32[]{:S(2)}, u32[]{:S(2)}) async-start(f32[32,56,128]{2,1,0:T(8,128)} %bitcast.5), calls=%async_computation.2 | async-start | bytes 1835008 | tf_op jit(solution)/shard_map/all_to_all | solution.py:514
  40.8 22.2 %copy-start = (f32[384,2,128]{2,1,0:T(2,128)S(1)}, f32[384,2,128]{2,1,0:T(2,128)}, u32[]{:S(2)}) copy-start(f32[384,2,128]{2,1,0:T(2,128)} %param.13) | copy-start | bytes 1179652
  40.8 22.2 %copy-start.1 = (s32[384,128]{1,0:T(8,128)S(1)}, s32[384,128]{1,0:T(8,128)}, u32[]{:S(2)}) copy-start(s32[384,128]{1,0:T(8,128)} %cell_ref.1) | copy-start | bytes 589828
  40.8 22.2 %copy-start.4 = (s32[384]{0:T(512)S(1)}, s32[384]{0:T(512)}, u32[]{:S(2)}) copy-start(s32[384]{0:T(512)} %chan_ref.1) | copy-start | bytes 4612
  53.2 9.8 %copy-start.2 = (s32[1,768]{1,0:T(1,128)S(1)}, s32[1,768]{1,0:T(1,128)}, u32[]{:S(2)}) copy-start(s32[1,768]{1,0:T(1,128)} %slot_ref.1) | copy-start | bytes 9220
  53.2 9.8 %copy-start.3 = (s32[384]{0:T(512)S(1)}, s32[384]{0:T(512)}, u32[]{:S(2)}) copy-start(s32[384]{0:T(512)} %count_ref.1) | copy-start | bytes 4612
  70.3 10.8 %collective-permute-start = (f32[16,256]{1,0:T(8,128)}, f32[16,256]{1,0:T(8,128)S(1)}, u32[]{:S(2)}, u32[]{:S(2)}) collective-permute-start(f32[16,256]{1,0:T(8,128)} %get-tuple-element.64), channel_id=1, source_target_pairs={{0,1},{1,0},{2,3},{3,2},{4,5},{5,4},{6,7},{7,6},{8,9},{9,8},{10,11... | collective-permute-start | bytes 49160 | tf_op jit(solution)/shard_map/ppermute | solution.py:533
  70.3 12.3 %collective-permute-start.1 = (f32[16,256]{1,0:T(8,128)}, f32[16,256]{1,0:T(8,128)S(1)}, u32[]{:S(2)}, u32[]{:S(2)}) collective-permute-start(f32[16,256]{1,0:T(8,128)} %get-tuple-element.65), channel_id=1, source_target_pairs={{0,3},{1,2},{2,1},{3,0},{4,7},{5,6},{6,5},{7,4},{8,11},{9,10},{10,... | collective-permute-start | bytes 49160 | tf_op jit(solution)/shard_map/ppermute | solution.py:534

commit v3 on v2

--- a/solution.py
+++ b/solution.py
@@ -35,10 +35,18 @@
     return -(-rows // 8) * 8
 
 
-def pack_kernel(sizes, wanted, slab_count, share, slot_ref, count_ref, chan_ref, cell_ref, offset_ref, center_ref,
-                width_ref, lum_ref, *refs):
-    outs = dict(zip(wanted, refs))
-    props, stream, slots, counts, chans, plan, moves, sem = refs[len(wanted) :]
+def pack_kernel(sizes, wanted, slab_count, share, slot_ref, count_ref, chan_ref, *refs):
+    inputs, refs = refs[:5], refs[5:]
+    sent, refs = refs[: len(wanted)], refs[len(wanted) :]
+    staged, refs = refs[: len(wanted)], refs[len(wanted) :]
+    props, stream, slots, counts, chans, plan, moves, sem = refs[:8]
+    refs = refs[8:]
+    (cell_ref, offset_ref, center_ref, width_ref, lum_ref), in_sem = refs[:5], refs[5]
+    out_sems = refs[6:]
+    outs = dict(zip(wanted, staged))
+    fetches = [pltpu.make_async_copy(a, b, in_sem.at[i]) for i, (a, b) in enumerate(zip(inputs, refs[:5]))]
+    for fetch_in in fetches:
+        fetch_in.start()
     dest_count = slots.shape[0]
     per_dest = sum(sizes)
     block_total = cell_ref.shape[0]
@@ -92,11 +100,21 @@
             props[pl.ds(8 * first + field, 8, stride=8), :] = values
         return carry
 
+    for fetch_in in fetches:
+        fetch_in.wait()
     lax.fori_loop(0, block_total // 8, gather_fields, 0, unroll=2)
     copy.wait()
+
+    def send(dest):
+        for out, whole, out_sem in zip(staged, sent, out_sems):
+            rows = out.shape[0] // dest_count
+            here = pl.ds(pl.multiple_of(dest * rows, 8), rows)
+            pltpu.make_async_copy(out.at[here], whole.at[here], out_sem).start()
+
     lanes = lax.broadcasted_iota(jnp.int32, (8, ROWS), 1)
 
     def one_dest(dest, carry):
+        pl.when(dest > 0)(lambda: send(dest - 1))
         for slot in range(per_dest):
             row, shift, target = (moves[dest, k * per_dest + slot] for k in range(3))
             row, target = pl.multiple_of(row, 8), pl.multiple_of(target, 8)
@@ -114,17 +132,23 @@
         return carry
 
     lax.fori_loop(0, dest_count, one_dest, 0)
+    send(dest_count - 1)
+    for out, whole, out_sem in zip(staged, sent, out_sems):
+        pltpu.make_async_copy(out, whole, out_sem).wait()
 
 
 def pack(sizes, wanted, dest_count, slab_count, share, slot_list, counts, chans, cells, offsets, centers, widths, lums):
     rows = [padded_rows(size * FIELDS + (2 if part == 0 else 0)) for part, size in enumerate(sizes)]
     block_total = cells.shape[0]
+    lists = (cells, offsets.reshape(block_total * 2, ROWS), centers, widths, lums)
+    shapes = [(dest_count * rows[part], ROWS) for part in wanted]
     sent = pl.pallas_call(
         functools.partial(pack_kernel, sizes, wanted, slab_count, share),
-        out_shape=[jax.ShapeDtypeStruct((dest_count * rows[part], ROWS), jnp.float32) for part in wanted],
-        in_specs=[VMEM] * 8,
-        out_specs=[VMEM] * len(wanted),
-        scratch_shapes=[
+        out_shape=[jax.ShapeDtypeStruct(shape, jnp.float32) for shape in shapes],
+        in_specs=[VMEM] * 3 + [ANY] * 5,
+        out_specs=[ANY] * len(wanted),
+        scratch_shapes=[pltpu.VMEM(shape, jnp.float32) for shape in shapes]
+        + [
             pltpu.VMEM((block_total * 8, ROWS), jnp.float32),
             pltpu.VMEM(((sum(sizes) + 2) * 8, ROWS), jnp.float32),
             pltpu.VMEM((dest_count, ROWS), jnp.int32),
@@ -133,12 +157,12 @@
             pltpu.VMEM((dest_count, ROWS), jnp.int32),
             pltpu.SMEM((dest_count, ROWS), jnp.int32),
             pltpu.SemaphoreType.DMA,
-        ],
+        ]
+        + [pltpu.VMEM(values.shape, values.dtype) for values in lists]
+        + [pltpu.SemaphoreType.DMA((5,))]
+        + [pltpu.SemaphoreType.DMA] * len(wanted),
         name="pack",
-    )(
-        slot_list, counts, chans, cells,
-        offsets.reshape(block_total * 2, ROWS), centers, widths, lums,
-    )
+    )(slot_list, counts, chans, *lists)
     return [piece.reshape(dest_count, rows[part], ROWS) for part, piece in zip(wanted, sent)]
 
 
@@ -406,7 +430,7 @@
     edge = jax.ShapeDtypeStruct((EDGE, PIX), jnp.float32)
     return pl.pallas_call(
         functools.partial(last_kernel, size, first, per_dest),
-        out_shape=[jax.ShapeDtypeStruct((PIX, share * CB), jnp.float32), edge, edge],
+        out_shape=[pltpu.VMEM((PIX, share * CB), jnp.float32), edge, edge],
         in_specs=[VMEM] * 3 + [ANY] * 2,
         out_specs=[VMEM] * 3,
         scratch_shapes=[
@@ -442,9 +466,7 @@
     return split(band)
 
 
-def taps_kernel(wide, taps_ref, cube_hbm, near_ref, far_ref, out_ref, cube_ref, out, high_ref, low_ref, sem, sems):
-    fetched = pltpu.make_async_copy(cube_hbm, cube_ref, sem)
-    fetched.start()
+def taps_kernel(wide, taps_ref, cube_ref, near_ref, far_ref, out_ref, out, high_ref, low_ref, sems):
     slab, last = lax.axis_index("slab"), lax.axis_size("slab") - 1
     even = lax.rem(slab, 2) == 0
     for ref, part in zip((high_ref, low_ref), band_part(taps_ref, -CB, 3 * CB)):
@@ -453,7 +475,6 @@
             ref[i : i + 3 * CB, i : i + CB] = part
     end = cube_ref.shape[1]
     copies = []
-    fetched.wait()
     for start in range(0, end, wide):
         low, high = max(start - CB, 0), min(start + wide + CB, end)
         rows, columns = slice(low - start + CB, high - start + CB), slice(start, start + wide)
@@ -472,15 +493,15 @@
 
 def sum_taps(taps, cube, near, far):
     wide = 2 * CB if cube.shape[1] % (2 * CB) == 0 else CB
-    near, far = (pltpu.with_memory_space_constraint(x, pltpu.VMEM) for x in (near, far))
+    cube, near, far = (pltpu.with_memory_space_constraint(x, pltpu.VMEM) for x in (cube, near, far))
     return pl.pallas_call(
         functools.partial(taps_kernel, wide),
         out_shape=jax.ShapeDtypeStruct(cube.shape, jnp.float32),
-        in_specs=[SMEM, ANY, VMEM, VMEM],
+        in_specs=[SMEM, VMEM, VMEM, VMEM],
         out_specs=ANY,
-        scratch_shapes=[pltpu.VMEM(cube.shape, jnp.float32)] * 2
+        scratch_shapes=[pltpu.VMEM(cube.shape, jnp.float32)]
         + [pltpu.VMEM((wide + 2 * CB, wide), jnp.bfloat16)] * 2
-        + [pltpu.SemaphoreType.DMA, pltpu.SemaphoreType.DMA((cube.shape[1] // wide,))],
+        + [pltpu.SemaphoreType.DMA((cube.shape[1] // wide,))],
         name="taps",
     )(taps, cube, near, far)
 

time: 87.7 us -> 86.2 us (0.983)
  the two profiles are of different devices: /device:TPU:17 before, /device:TPU:1 now
where the time goes in v3:
time: 86.2 us; the launch traced here: 84.9 us
  Pallas kernels  45 us (52%)
  blocking collectives  29.7 us (34%)
  starting transfers between devices  6.31 us (7%)
  waiting for transfers between devices  2.03 us (2%)
    all_to_all x1, blocking collectives, exchange(): lax.all_to_all(piece, ('tile', 'slab'), split_axis=0, concat_axis=0, tile...  29.7 us
    pallas_call x1, Pallas kernels, deposit_first(): pl.pallas_call(functools.partial(first_kernel, size, per_dest, share), ou...  20.9 us
    pallas_call x1, Pallas kernels, deposit_last(): pl.pallas_call(functools.partial(last_kernel, size, first, per_dest), out...  14.6 us
    pallas_call x1, Pallas kernels, pack(): pl.pallas_call(functools.partial(pack_kernel, sizes, wanted, slab_count,...  6.91 us
    all_to_all x1, starting transfers between devices, exchange(): lax.all_to_all(piece, ('tile', 'slab'), split_axis=0, concat_axis=0, tile...  4.39 us
    pallas_call x1, Pallas kernels, sum_taps(): pl.pallas_call(functools.partial(taps_kernel, wide), out_shape=jax.ShapeD...  2.69 us
    ppermute x1, starting transfers between devices, body(): lax.ppermute(far, 'slab', [(i, (i + 1 if i % 2 else i - 1) % slab_count)...  1.85 us
  transfers between devices with their start and end apart: 3, of which 2 were waited for; matrix products, arithmetic and copies ran while one was open for 1% of the time, Pallas kernels for 25%

profile of v3, /device:TPU:1, one launch (start us, length us, event | category | flops | bytes accessed | tf_op | source)
XLA Modules:
  0.0 84.9 jit_solution(763544471306467518)
XLA Ops:
  0.0 6.9 %pack.3 = (f32[1792,128]{1,0:T(8,128)}, f32[1792,128]{1,0:T(8,128)}) custom-call(s32[1,768]{1,0:T(1,128)} %slot_ref.1, s32[384]{0:T(512)} %count_ref.1, s32[384]{0:T(512)} %chan_ref.1, s32[384,128]{1,0:T(8,128)} %refs_0_.1, f32[768,128]{1,0:T(8,128)} %bitcast.14, f32[384,128]{1,0:T(8,128)} %refs_2_.1, f32[384,128]{1,0:T(8,128)} %refs_3_.1, f32[384,128]{1,0:T(8,128)} %refs_4_.1), custom_call_target="tpu_custom_call" | custom-call | tf_op jit(solution)/shard_map/pack/pallas_call | solution.py:145
  6.9 29.7 %all_to_all.15 = f32[32,56,128]{2,1,0:T(8,128)S(1)} all-to-all(f32[32,56,128]{2,1,0:T(8,128)} %bitcast.16), channel_id=1, replica_groups=mesh['tile'=8,'slab'=4] {'tile','slab'}, dimensions={0} | all-to-all | bytes 1835008 | tf_op jit(solution)/shard_map/all_to_all | solution.py:535
  36.6 4.4 %all-to-all-start.2 = ((f32[32,56,128]{2,1,0:T(8,128)}), f32[32,56,128]{2,1,0:T(8,128)S(1)}, u32[]{:S(2)}, u32[]{:S(2)}) async-start(f32[32,56,128]{2,1,0:T(8,128)} %bitcast.5), calls=%async_computation.2 | async-start | bytes 1835008 | tf_op jit(solution)/shard_map/all_to_all | solution.py:535
  41.0 0.0 copy-start
  41.1 0.0 copy-start.1
  41.1 0.0 copy-start.4
  41.1 20.9 %deposit_first.1 = (f32[8,256,128]{2,1,0:T(8,128)S(1)}, f32[32,128]{1,0:T(8,128)S(1)}, f32[32,128]{1,0:T(8,128)S(1)}) custom-call(f32[1792,128]{1,0:T(8,128)S(1)} %bitcast.12), custom_call_target="tpu_custom_call" | custom-call | flops 2415919104 | bytes 917504 | tf_op jit(solution)/shard_map/deposit_first/pallas_call | solution.py:405
  62.0 0.7 slice_reduce_fusion
  63.3 0.0 copy-start.2
  63.3 0.0 copy-start.3
  63.3 0.4 all-to-all-done.2
  63.7 0.0 copy-done
  63.7 0.0 copy-done.1
  63.7 0.0 copy-done.4
  63.7 0.3 copy-done.2
  64.0 0.0 copy-done.3
  64.0 14.6 %deposit_last.1 = (f32[256,1024]{1,0:T(8,128)S(1)}, f32[16,256]{1,0:T(8,128)}, f32[16,256]{1,0:T(8,128)}) custom-call(f32[32,128]{1,0:T(8,128)S(1)} %get-tuple-element.57.chan_ref, f32[32,128]{1,0:T(8,128)S(1)} %get-tuple-element.58.end_ref, f32[1,1024]{1,0:T(1,128)} %bitcast.17, f32[1792,128]{1,0:T(8,128)S(1)} %bitcast.11, ...), custom_call_target="tpu_custom_call" | custom-call | flops 2415919104 | bytes 917504 | tf_op jit(solution)/shard_map/deposit_last/pallas_call | solution.py:431
  78.6 0.1 collective-permute-start
  78.6 1.9 %collective-permute-start.1 = (f32[16,256]{1,0:T(8,128)}, f32[16,256]{1,0:T(8,128)S(1)}, u32[]{:S(2)}, u32[]{:S(2)}) collective-permute-start(f32[16,256]{1,0:T(8,128)} %get-tuple-element.65), channel_id=1, source_target_pairs={{0,3},{1,2},{2,1},{3,0},{4,7},{5,6},{6,5},{7,4},{8,11},{9,10},{10,... | collective-permute-start | bytes 49160 | tf_op jit(solution)/shard_map/ppermute | solution.py:555
  80.5 0.0 collective-permute-done.near_ref
  80.5 1.7 %collective-permute-done.1.far_ref = f32[16,256]{1,0:T(8,128)S(1)} collective-permute-done((f32[16,256]{1,0:T(8,128)}, f32[16,256]{1,0:T(8,128)S(1)}, u32[]{:S(2)}, u32[]{:S(2)}) %collective-permute-start.1) | collective-permute-done | bytes 16416 | tf_op jit(solution)/shard_map/ppermute | solution.py:555
  82.2 2.7 %taps.1 = f32[256,1024]{1,0:T(8,128)} custom-call(f32[31]{0:T(128)} %taps_ref.1, f32[256,1024]{1,0:T(8,128)S(1)} %get-tuple-element.63.cube_ref, f32[16,256]{1,0:T(8,128)S(1)} %collective-permute-done.near_ref, f32[16,256]{1,0:T(8,128)S(1)} %collective-permute-done.1.far_ref), custom_call_target="tpu_custom_call" | custom-call | tf_op jit(solution)/shard_map/taps/pallas_call | solution.py:497
  (1 shorter events, 0.0 us)
Async XLA Ops:
  36.6 27.0 %all-to-all-start.2 = ((f32[32,56,128]{2,1,0:T(8,128)}), f32[32,56,128]{2,1,0:T(8,128)S(1)}, u32[]{:S(2)}, u32[]{:S(2)}) async-start(f32[32,56,128]{2,1,0:T(8,128)} %bitcast.5), calls=%async_computation.2 | async-start | bytes 1835008 | tf_op jit(solution)/shard_map/all_to_all | solution.py:535
  41.0 22.6 %copy-start = (f32[384,2,128]{2,1,0:T(2,128)S(1)}, f32[384,2,128]{2,1,0:T(2,128)}, u32[]{:S(2)}) copy-start(f32[384,2,128]{2,1,0:T(2,128)} %param.13) | copy-start | bytes 1179652
  41.1 22.6 %copy-start.1 = (s32[384,128]{1,0:T(8,128)S(1)}, s32[384,128]{1,0:T(8,128)}, u32[]{:S(2)}) copy-start(s32[384,128]{1,0:T(8,128)} %refs_0_.1) | copy-start | bytes 589828
  41.1 22.6 %copy-start.4 = (s32[384]{0:T(512)S(1)}, s32[384]{0:T(512)}, u32[]{:S(2)}) copy-start(s32[384]{0:T(512)} %chan_ref.1) | copy-start | bytes 4612
  63.3 0.7 copy-start.2
  63.3 0.7 copy-start.3
  78.6 1.9 %collective-permute-start = (f32[16,256]{1,0:T(8,128)}, f32[16,256]{1,0:T(8,128)S(1)}, u32[]{:S(2)}, u32[]{:S(2)}) collective-permute-start(f32[16,256]{1,0:T(8,128)} %get-tuple-element.64), channel_id=1, source_target_pairs={{0,1},{1,0},{2,3},{3,2},{4,5},{5,4},{6,7},{7,6},{8,9},{9,8},{10,11... | collective-permute-start | bytes 49160 | tf_op jit(solution)/shard_map/ppermute | solution.py:554
  78.6 3.5 %collective-permute-start.1 = (f32[16,256]{1,0:T(8,128)}, f32[16,256]{1,0:T(8,128)S(1)}, u32[]{:S(2)}, u32[]{:S(2)}) collective-permute-start(f32[16,256]{1,0:T(8,128)} %get-tuple-element.65), channel_id=1, source_target_pairs={{0,3},{1,2},{2,1},{3,0},{4,7},{5,6},{6,5},{7,4},{8,11},{9,10},{10,... | collective-permute-start | bytes 49160 | tf_op jit(solution)/shard_map/ppermute | solution.py:555

commit v4 on v3

--- a/solution.py
+++ b/solution.py
@@ -19,6 +19,7 @@
 FIELDS = 6
 UNROLL = 6
 SKIP = 8
+AHEAD = 4
 LOG2E = math.log2(math.e)
 SMEM = pl.BlockSpec(memory_space=pltpu.SMEM)
 VMEM = pl.BlockSpec(memory_space=pltpu.VMEM)
@@ -39,8 +40,8 @@
     inputs, refs = refs[:5], refs[5:]
     sent, refs = refs[: len(wanted)], refs[len(wanted) :]
     staged, refs = refs[: len(wanted)], refs[len(wanted) :]
-    props, stream, slots, counts, chans, plan, moves, sem = refs[:8]
-    refs = refs[8:]
+    props, *streams, slots, counts, chans, plan, moves, sem = refs[: 7 + AHEAD]
+    refs = refs[7 + AHEAD :]
     (cell_ref, offset_ref, center_ref, width_ref, lum_ref), in_sem = refs[:5], refs[5]
     out_sems = refs[6:]
     outs = dict(zip(wanted, staged))
@@ -113,25 +114,32 @@
 
     lanes = lax.broadcasted_iota(jnp.int32, (8, ROWS), 1)
 
-    def one_dest(dest, carry):
-        pl.when(dest > 0)(lambda: send(dest - 1))
+    def some_dests(turn, carry):
+        first = turn * len(streams)
+        for back in range(len(streams)):
+            pl.when(turn > 0)(functools.partial(send, first - 1 - back))
         for slot in range(per_dest):
-            row, shift, target = (moves[dest, k * per_dest + slot] for k in range(3))
-            row, target = pl.multiple_of(row, 8), pl.multiple_of(target, 8)
-            turned = pltpu.roll(props[pl.ds(row, 8), :], shift, 1)
-            pltpu.store(stream.at[pl.ds(target, 8), :], turned, mask=lanes >= shift)
-            stream[pl.ds(target + 8, 8), :] = turned
-        group = 0
-        for part, size in enumerate(sizes):
-            if part in outs:
-                out = outs[part]
-                base = pl.multiple_of(dest * (out.shape[0] // dest_count), 8)
-                for place in range(size):
-                    out[pl.ds(base + place * FIELDS, FIELDS), :] = stream[8 * (group + place) : 8 * (group + place) + FIELDS, :]
-            group += size
+            for ahead, stream in enumerate(streams):
+                row, shift, target = (moves[first + ahead, k * per_dest + slot] for k in range(3))
+                row, target = pl.multiple_of(row, 8), pl.multiple_of(target, 8)
+                turned = pltpu.roll(props[pl.ds(row, 8), :], shift, 1)
+                pltpu.store(stream.at[pl.ds(target, 8), :], turned, mask=lanes >= shift)
+                stream[pl.ds(target + 8, 8), :] = turned
+        for ahead, stream in enumerate(streams):
+            group = 0
+            for part, size in enumerate(sizes):
+                if part in outs:
+                    out = outs[part]
+                    base = pl.multiple_of((first + ahead) * (out.shape[0] // dest_count), 8)
+                    for place in range(size):
+                        here = 8 * (group + place)
+                        out[pl.ds(base + place * FIELDS, FIELDS), :] = stream[here : here + FIELDS, :]
+                group += size
         return carry
 
-    lax.fori_loop(0, dest_count, one_dest, 0)
+    lax.fori_loop(0, dest_count // len(streams), some_dests, 0)
+    for back in range(1, len(streams)):
+        send(dest_count - 1 - back)
     send(dest_count - 1)
     for out, whole, out_sem in zip(staged, sent, out_sems):
         pltpu.make_async_copy(out, whole, out_sem).wait()
@@ -150,7 +158,7 @@
         scratch_shapes=[pltpu.VMEM(shape, jnp.float32) for shape in shapes]
         + [
             pltpu.VMEM((block_total * 8, ROWS), jnp.float32),
-            pltpu.VMEM(((sum(sizes) + 2) * 8, ROWS), jnp.float32),
+            *[pltpu.VMEM(((sum(sizes) + 2) * 8, ROWS), jnp.float32)] * AHEAD,
             pltpu.VMEM((dest_count, ROWS), jnp.int32),
             pltpu.VMEM((dest_count, ROWS), jnp.float32),
             pltpu.VMEM((dest_count, ROWS), jnp.float32),

time: 86.2 us -> 85 us (0.986)
  Pallas kernels: 45 us -> 29.6 us
  starting transfers between devices: 6.31 us -> 14.2 us
  waiting for transfers between devices: 2.03 us -> 8.8 us
    pallas_call x1, Pallas kernels: 14.6 us -> 6.94 us  [deposit_last(): pl.pallas_call(functools.partial(last_kernel, size, first, per_dest), out...]
    ppermute x1, starting transfers between devices: 1.85 us -> 8.73 us  [body(): lax.ppermute(far, 'slab', [(i, (i + 1 if i % 2 else i - 1) % slab_count)...]
    all_to_all x1, waiting for transfers between devices: 0.36 us -> 7.13 us  [exchange(): lax.all_to_all(piece, ('tile', 'slab'), split_axis=0, concat_axis=0, tile...]
    pallas_call x1, Pallas kernels: 20.9 us -> 14.1 us  [deposit_first(): pl.pallas_call(functools.partial(first_kernel, size, per_dest, share), ou...]
    pallas_call x1, Pallas kernels: 6.91 us -> 5.84 us  [pack(): pl.pallas_call(functools.partial(pack_kernel, sizes, wanted, slab_count,...]
    ppermute x1, starting transfers between devices: 0.07 us -> 1.09 us  [body(): near = lax.ppermute(near, 'slab', [(i, i ^ 1) for i in range(slab_count)])]
  transfers between devices with their start and end apart: 3 -> 3, of which waited for: 2 -> 2; matrix products, arithmetic and copies ran while one was open for 1% -> 1% of each run, Pallas kernels for 25% -> 17%
where the time goes in v4:
time: 85 us; the launch traced here: 83.8 us
  blocking collectives  29.7 us (35%)
  Pallas kernels  29.6 us (35%)
  starting transfers between devices  14.2 us (17%)
  waiting for transfers between devices  8.8 us (10%)
    all_to_all x1, blocking collectives, exchange(): lax.all_to_all(piece, ('tile', 'slab'), split_axis=0, concat_axis=0, tile...  29.7 us
    pallas_call x1, Pallas kernels, deposit_first(): pl.pallas_call(functools.partial(first_kernel, size, per_dest, share), ou...  14.1 us
    ppermute x1, starting transfers between devices, body(): lax.ppermute(far, 'slab', [(i, (i + 1 if i % 2 else i - 1) % slab_count)...  8.73 us
    all_to_all x1, waiting for transfers between devices, exchange(): lax.all_to_all(piece, ('tile', 'slab'), split_axis=0, concat_axis=0, tile...  7.13 us
    pallas_call x1, Pallas kernels, deposit_last(): pl.pallas_call(functools.partial(last_kernel, size, first, per_dest), out...  6.94 us
    pallas_call x1, Pallas kernels, pack(): pl.pallas_call(functools.partial(pack_kernel, sizes, wanted, slab_count,...  5.84 us
    all_to_all x1, starting transfers between devices, exchange(): lax.all_to_all(piece, ('tile', 'slab'), split_axis=0, concat_axis=0, tile...  4.39 us
    pallas_call x1, Pallas kernels, sum_taps(): pl.pallas_call(functools.partial(taps_kernel, wide), out_shape=jax.ShapeD...  2.69 us
  transfers between devices with their start and end apart: 3, of which 2 were waited for; matrix products, arithmetic and copies ran while one was open for 1% of the time, Pallas kernels for 17%

profile of v4, /device:TPU:1, one launch (start us, length us, event | category | flops | bytes accessed | tf_op | source)
XLA Modules:
  0.0 83.8 jit_solution(10011383883539180728)
XLA Ops:
  0.0 5.8 %pack.3 = (f32[1792,128]{1,0:T(8,128)}, f32[1792,128]{1,0:T(8,128)}) custom-call(s32[1,768]{1,0:T(1,128)} %slot_ref.1, s32[384]{0:T(512)} %count_ref.1, s32[384]{0:T(512)} %chan_ref.1, s32[384,128]{1,0:T(8,128)} %refs_0_.1, f32[768,128]{1,0:T(8,128)} %bitcast.14, f32[384,128]{1,0:T(8,128)} %refs_2_.1, f32[384,128]{1,0:T(8,128)} %refs_3_.1, f32[384,128]{1,0:T(8,128)} %refs_4_.1), custom_call_target="tpu_custom_call" | custom-call | tf_op jit(solution)/shard_map/pack/pallas_call | solution.py:153
  5.8 29.7 %all_to_all.15 = f32[32,56,128]{2,1,0:T(8,128)S(1)} all-to-all(f32[32,56,128]{2,1,0:T(8,128)} %bitcast.16), channel_id=1, replica_groups=mesh['tile'=8,'slab'=4] {'tile','slab'}, dimensions={0} | all-to-all | bytes 1835008 | tf_op jit(solution)/shard_map/all_to_all | solution.py:543
  35.6 4.4 %all-to-all-start.2 = ((f32[32,56,128]{2,1,0:T(8,128)}), f32[32,56,128]{2,1,0:T(8,128)S(1)}, u32[]{:S(2)}, u32[]{:S(2)}) async-start(f32[32,56,128]{2,1,0:T(8,128)} %bitcast.5), calls=%async_computation.2 | async-start | bytes 1835008 | tf_op jit(solution)/shard_map/all_to_all | solution.py:543
  40.0 0.0 copy-start
  40.0 0.0 copy-start.1
  40.0 0.0 copy-start.4
  40.0 14.1 %deposit_first.1 = (f32[8,256,128]{2,1,0:T(8,128)S(1)}, f32[32,128]{1,0:T(8,128)S(1)}, f32[32,128]{1,0:T(8,128)S(1)}) custom-call(f32[1792,128]{1,0:T(8,128)S(1)} %bitcast.12), custom_call_target="tpu_custom_call" | custom-call | flops 2415919104 | bytes 917504 | tf_op jit(solution)/shard_map/deposit_first/pallas_call | solution.py:413
  54.1 0.7 slice_reduce_fusion
  55.4 0.0 copy-start.2
  55.5 0.0 copy-start.3
  55.5 7.1 %all-to-all-done.2 = f32[32,56,128]{2,1,0:T(8,128)S(1)} async-done(((f32[32,56,128]{2,1,0:T(8,128)}), f32[32,56,128]{2,1,0:T(8,128)S(1)}, u32[]{:S(2)}, u32[]{:S(2)}) %all-to-all-start.2) | async-done | bytes 917536 | tf_op jit(solution)/shard_map/all_to_all | solution.py:543
  62.6 0.0 copy-done
  62.6 0.0 copy-done.1
  62.6 0.0 copy-done.4
  62.6 0.0 copy-done.2
  62.6 0.0 copy-done.3
  62.6 6.9 %deposit_last.1 = (f32[256,1024]{1,0:T(8,128)S(1)}, f32[16,256]{1,0:T(8,128)}, f32[16,256]{1,0:T(8,128)}) custom-call(f32[32,128]{1,0:T(8,128)S(1)} %get-tuple-element.57.chan_ref, f32[32,128]{1,0:T(8,128)S(1)} %get-tuple-element.58.end_ref, f32[1,1024]{1,0:T(1,128)} %bitcast.17, f32[1792,128]{1,0:T(8,128)S(1)} %bitcast.11, ...), custom_call_target="tpu_custom_call" | custom-call | flops 2415919104 | bytes 917504 | tf_op jit(solution)/shard_map/deposit_last/pallas_call | solution.py:439
  69.6 1.1 %collective-permute-start = (f32[16,256]{1,0:T(8,128)}, f32[16,256]{1,0:T(8,128)S(1)}, u32[]{:S(2)}, u32[]{:S(2)}) collective-permute-start(f32[16,256]{1,0:T(8,128)} %get-tuple-element.64), channel_id=1, source_target_pairs={{0,1},{1,0},{2,3},{3,2},{4,5},{5,4},{6,7},{7,6},{8,9},{9,8},{10,11... | collective-permute-start | bytes 49160 | tf_op jit(solution)/shard_map/ppermute | solution.py:562
  70.7 8.7 %collective-permute-start.1 = (f32[16,256]{1,0:T(8,128)}, f32[16,256]{1,0:T(8,128)S(1)}, u32[]{:S(2)}, u32[]{:S(2)}) collective-permute-start(f32[16,256]{1,0:T(8,128)} %get-tuple-element.65), channel_id=1, source_target_pairs={{0,3},{1,2},{2,1},{3,0},{4,7},{5,6},{6,5},{7,4},{8,11},{9,10},{10,... | collective-permute-start | bytes 49160 | tf_op jit(solution)/shard_map/ppermute | solution.py:563
  79.4 0.0 collective-permute-done.near_ref
  79.4 1.7 %collective-permute-done.1.far_ref = f32[16,256]{1,0:T(8,128)S(1)} collective-permute-done((f32[16,256]{1,0:T(8,128)}, f32[16,256]{1,0:T(8,128)S(1)}, u32[]{:S(2)}, u32[]{:S(2)}) %collective-permute-start.1) | collective-permute-done | bytes 16416 | tf_op jit(solution)/shard_map/ppermute | solution.py:563
  81.1 2.7 %taps.1 = f32[256,1024]{1,0:T(8,128)} custom-call(f32[31]{0:T(128)} %taps_ref.1, f32[256,1024]{1,0:T(8,128)S(1)} %get-tuple-element.63.cube_ref, f32[16,256]{1,0:T(8,128)S(1)} %collective-permute-done.near_ref, f32[16,256]{1,0:T(8,128)S(1)} %collective-permute-done.1.far_ref), custom_call_target="tpu_custom_call" | custom-call | tf_op jit(solution)/shard_map/taps/pallas_call | solution.py:505
  (1 shorter events, 0.0 us)
Async XLA Ops:
  35.6 27.0 %all-to-all-start.2 = ((f32[32,56,128]{2,1,0:T(8,128)}), f32[32,56,128]{2,1,0:T(8,128)S(1)}, u32[]{:S(2)}, u32[]{:S(2)}) async-start(f32[32,56,128]{2,1,0:T(8,128)} %bitcast.5), calls=%async_computation.2 | async-start | bytes 1835008 | tf_op jit(solution)/shard_map/all_to_all | solution.py:543
  40.0 22.6 %copy-start = (f32[384,2,128]{2,1,0:T(2,128)S(1)}, f32[384,2,128]{2,1,0:T(2,128)}, u32[]{:S(2)}) copy-start(f32[384,2,128]{2,1,0:T(2,128)} %param.13) | copy-start | bytes 1179652
  40.0 22.6 %copy-start.1 = (s32[384,128]{1,0:T(8,128)S(1)}, s32[384,128]{1,0:T(8,128)}, u32[]{:S(2)}) copy-start(s32[384,128]{1,0:T(8,128)} %refs_0_.1) | copy-start | bytes 589828
  40.0 22.6 %copy-start.4 = (s32[384]{0:T(512)S(1)}, s32[384]{0:T(512)}, u32[]{:S(2)}) copy-start(s32[384]{0:T(512)} %chan_ref.1) | copy-start | bytes 4612
  55.4 7.2 %copy-start.2 = (s32[1,768]{1,0:T(1,128)S(1)}, s32[1,768]{1,0:T(1,128)}, u32[]{:S(2)}) copy-start(s32[1,768]{1,0:T(1,128)} %slot_ref.1) | copy-start | bytes 9220
  55.5 7.2 %copy-start.3 = (s32[384]{0:T(512)S(1)}, s32[384]{0:T(512)}, u32[]{:S(2)}) copy-start(s32[384]{0:T(512)} %count_ref.1) | copy-start | bytes 4612
  69.6 9.8 %collective-permute-start = (f32[16,256]{1,0:T(8,128)}, f32[16,256]{1,0:T(8,128)S(1)}, u32[]{:S(2)}, u32[]{:S(2)}) collective-permute-start(f32[16,256]{1,0:T(8,128)} %get-tuple-element.64), channel_id=1, source_target_pairs={{0,1},{1,0},{2,3},{3,2},{4,5},{5,4},{6,7},{7,6},{8,9},{9,8},{10,11... | collective-permute-start | bytes 49160 | tf_op jit(solution)/shard_map/ppermute | solution.py:562
  70.7 10.4 %collective-permute-start.1 = (f32[16,256]{1,0:T(8,128)}, f32[16,256]{1,0:T(8,128)S(1)}, u32[]{:S(2)}, u32[]{:S(2)}) collective-permute-start(f32[16,256]{1,0:T(8,128)} %get-tuple-element.65), channel_id=1, source_target_pairs={{0,3},{1,2},{2,1},{3,0},{4,7},{5,6},{6,5},{7,4},{8,11},{9,10},{10,... | collective-permute-start | bytes 49160 | tf_op jit(solution)/shard_map/ppermute | solution.py:563
